TPU v7x, 128 devices: a whole 4x4x4 slice. The times are simulated.
128 devices in a mesh: grp: 8 (over x, core), dev: 16 (over y, z).
Axes of the slice: x: 4, y: 4, z: 4, core: 2. Of those that a mesh axis runs over, the one named last changes fastest.
Arguments:
- parent_state: float32 [24, 512, 2048], P(None, 'grp', 'dev'), may hold values from -6 to 6
- nest_state: float32 [16, 24, 384, 384], P('grp', None, 'dev'), may hold values from -6 to 6
- nest_anchor: int32 [16, 2], replicated, may hold values from 0 to 1920, as said below
- diffusion: float32 [2, 24], replicated, may hold values from 0.02 to 0.05
- courant: float32 [2, 24], replicated, may hold values from 0.05 to 0.15
Outputs:
- parent_out: float32 [24, 512, 2048], P(None, 'grp', 'dev')
- nest_out: float32 [16, 24, 384, 384], P('grp', None, 'dev')
Inputs may be any that keep to these rules, and one draw needn't show every extreme that they name: `nest_anchor`: the parent grid is cut into 2 x 16 / 2 disjoint bands of 256 x 256 cells; each nest lies in a band of its own, its 128 x 128 covered cells inside that band.
All inputs are finite; a program needn't handle non-finite values.
Results may differ from a plain program's by a relative error of at most 0.0003.
Values sent between devices are 32-bit elements; how exact they have to be, the bound alone decides.
A program may use at most 320 MiB of HBM per device.

v0:
```python
import jax
import jax.numpy as jnp
from jax import lax
from jax.sharding import PartitionSpec as P


def padded_2(shard, sides, width):
    for axis, dim in sides:
        size, length = (lax.axis_size(axis), shard.shape[dim])
        up = [(i, (i + 1) % size) for i in range(size - 1)]
        down = [(j, i) for i, j in up]
        last = lax.slice_in_dim(shard, length - width, length, axis=dim)
        initial = lax.slice_in_dim(shard, 0, width, axis=dim)
        before = lax.ppermute(last, axis, up)
        after = lax.ppermute(initial, axis, down)
        shard = jnp.concatenate([before, shard, after], axis=dim)
    return shard


def stencil(padded, diff_x, diff_y, adv_x, adv_y):
    centre = padded[..., 1:-1, 1:-1]
    eastern = padded[..., 1:-1, 2:]
    western = padded[..., 1:-1, :-2]
    northern = padded[..., 2:, 1:-1]
    southern = padded[..., :-2, 1:-1]
    return (
        centre
        + diff_x * (eastern - 2.0 * centre + western)
        + diff_y * (northern - 2.0 * centre + southern)
        - adv_x * (centre - western)
        - adv_y * (centre - southern)
    )


def impose(extended, row_index, south_fine, north_fine, total_rows):
    below = (row_index < 0)[None, None, :, None]
    above = (row_index >= total_rows)[None, None, :, None]
    extended = jnp.where(below, south_fine[:, :, None, :], extended)
    return jnp.where(above, north_fine[:, :, None, :], extended)


def substep_once(
    extended, row_index, west_full, east_full, south_fine, north_fine, total_rows, coefficients
):
    row_count = extended.shape[2]
    first_row = row_index[0] + 3
    west_col = lax.dynamic_slice_in_dim(west_full, first_row, row_count, 2)
    east_col = lax.dynamic_slice_in_dim(east_full, first_row, row_count, 2)
    padded = jnp.concatenate([west_col[..., None], extended, east_col[..., None]], axis=3)
    advanced = stencil(padded, coefficients[0], coefficients[1], coefficients[2], coefficients[3])
    inner_rows = row_index[1:-1]
    return (impose(advanced, inner_rows, south_fine, north_fine, total_rows), inner_rows)


def shards(parent_state, nest_state, nest_anchor, diffusion, courant):
    channels, tile_rows, tile_cols = parent_state.shape
    local_nests = nest_state.shape[0]
    nest_rows_dev = nest_state.shape[2]
    fine_cols = nest_state.shape[3]
    dev_count = lax.axis_size("dev")
    grp_index = lax.axis_index("grp")
    dev_index = lax.axis_index("dev")
    total_rows = nest_rows_dev * dev_count
    foot_rows = total_rows // 3
    foot_cols = fine_cols // 3
    nest_count = nest_anchor.shape[0]
    diff_x = diffusion[0][:, None, None]
    diff_y = diffusion[1][:, None, None]
    adv_x = courant[0][:, None, None]
    adv_y = courant[1][:, None, None]
    nest_coefficients = (3.0 * diff_x, 3.0 * diff_y, adv_x, adv_y)
    row_base = grp_index * tile_rows
    col_base = dev_index * tile_cols
    highest = lax.Precision.HIGHEST
    row_anchor = nest_anchor[:, 0:1]
    col_anchor = nest_anchor[:, 1:2]
    along_rows = jnp.arange(foot_rows, dtype=jnp.int32)[None, :]
    along_cols = jnp.arange(foot_cols, dtype=jnp.int32)[None, :]
    rows_here = row_base + jnp.arange(tile_rows, dtype=jnp.int32)
    cols_here = col_base + jnp.arange(tile_cols, dtype=jnp.int32)
    side_cols = jnp.concatenate([col_anchor - 1, col_anchor + foot_cols], axis=0)
    column_pick = (side_cols == cols_here[None, :]).astype(jnp.float32)
    column_values = jnp.einsum("cyx,mx->cym", parent_state, column_pick, precision=highest)
    row_span = ((row_anchor + along_rows)[:, :, None] == rows_here[None, None, :]).astype(
        jnp.float32
    )
    west_part = jnp.einsum(
        "nky,cyn->cnk", row_span, column_values[:, :, :nest_count], precision=highest
    )
    east_part = jnp.einsum(
        "nky,cyn->cnk", row_span, column_values[:, :, nest_count:], precision=highest
    )
    side_rows = jnp.concatenate([row_anchor - 1, row_anchor + foot_rows], axis=0)
    row_pick = (side_rows == rows_here[None, :]).astype(jnp.float32)
    row_values = jnp.einsum("my,cyx->cmx", row_pick, parent_state, precision=highest)
    col_span = ((col_anchor + along_cols)[:, :, None] == cols_here[None, None, :]).astype(
        jnp.float32
    )
    south_part = jnp.einsum("nkx,cnx->cnk", col_span, row_values[:, :nest_count], precision=highest)
    north_part = jnp.einsum("nkx,cnx->cnk", col_span, row_values[:, nest_count:], precision=highest)
    contrib = jnp.concatenate([west_part, east_part, south_part, north_part], axis=2)
    cycle_every = lax.psum(contrib, ("grp", "dev"))
    cycle_local = lax.dynamic_slice_in_dim(cycle_every, grp_index * local_nests, local_nests, 1)
    cycle_local = jnp.swapaxes(cycle_local, 0, 1)
    west_fine = jnp.repeat(cycle_local[:, :, :foot_rows], 3, axis=2)
    east_fine = jnp.repeat(cycle_local[:, :, foot_rows : 2 * foot_rows], 3, axis=2)
    west_full = jnp.pad(west_fine, ((0, 0), (0, 0), (3, 3)), mode="edge")
    east_full = jnp.pad(east_fine, ((0, 0), (0, 0), (3, 3)), mode="edge")
    south_fine = jnp.repeat(cycle_local[:, :, 2 * foot_rows : 2 * foot_rows + foot_cols], 3, axis=2)
    north_fine = jnp.repeat(cycle_local[:, :, 2 * foot_rows + foot_cols :], 3, axis=2)
    parent_pad = padded_2(parent_state, (("grp", 1), ("dev", 2)), 1)
    advanced = stencil(parent_pad, diff_x, diff_y, adv_x, adv_y)
    current = nest_state
    for substep in range(3):
        extended = padded_2(current, (("dev", 2),), 1)
        row_index = dev_index * nest_rows_dev - 1 + jnp.arange(nest_rows_dev + 2, dtype=jnp.int32)
        extended = impose(extended, row_index, south_fine, north_fine, total_rows)
        current = substep_once(
            extended,
            row_index,
            west_full,
            east_full,
            south_fine,
            north_fine,
            total_rows,
            nest_coefficients,
        )[0]
    coarse_rows = nest_rows_dev // 3
    averages = current.reshape(local_nests, channels, coarse_rows, 3, foot_cols, 3).mean(
        axis=(3, 5)
    )
    per_group = local_nests * dev_count
    zero_start = jnp.zeros((), jnp.int32)
    canvas = jnp.pad(advanced, ((0, 0), (coarse_rows, coarse_rows), (foot_cols, foot_cols)))
    pieces = lax.all_gather(averages, ("grp", "dev"), axis=0, tiled=True)
    item_count = pieces.shape[0]

    def put_one(item, canvas_inner):
        group_index = item // per_group
        member = item // local_nests % dev_count
        nest_index = group_index * local_nests + item % local_nests
        anchor = lax.dynamic_slice(nest_anchor, (nest_index, zero_start), (1, 2))
        top_at = jnp.clip(
            anchor[0, 0] + member * coarse_rows - row_base + coarse_rows, 0, tile_rows + coarse_rows
        )
        left_at = jnp.clip(anchor[0, 1] - col_base + foot_cols, 0, tile_cols + foot_cols)
        piece = lax.dynamic_index_in_dim(pieces, item, 0, keepdims=False)
        return lax.dynamic_update_slice(canvas_inner, piece, (zero_start, top_at, left_at))

    filled = lax.fori_loop(0, item_count, put_one, canvas)
    parent_out = filled[:, coarse_rows : coarse_rows + tile_rows, foot_cols : foot_cols + tile_cols]
    return (parent_out, current)


def solution(mesh):
    placed = (P(None, "grp", "dev"), P("grp", None, "dev", None), P(), P(), P())
    return jax.shard_map(
        shards,
        mesh=mesh,
        in_specs=placed,
        out_specs=(P(None, "grp", "dev"), P("grp", None, "dev", None)),
        check_vma=False,
    )
```

profile of v0, /device:TPU:95, one launch (start us, length us, event | category | flops | bytes accessed | tf_op | source)
XLA Modules:
  0.0 2034.8 jit_solution(8243158186074569799)
XLA Ops:
  16.5 3.3 collective-permute-start.4
  22.1 138.1 %all-reduce.3.cloned.1.call-done = f32[24,16,512]{2,0,1:T(8,128)} async-done(((f32[24,16,512]{2,0,1:T(8,128)}), f32[24,16,512]{2,0,1:T(8,128)}) %all-reduce.3.cloned.1.call-update) | async-done | bytes 786448 | tf_op jit(solution)/shard_map/psum | solution.py:102
  180.6 3.7 collective-permute-start.9
  188.6 8.9 copy.162
  197.5 10.2 reduce_sum.9
  211.3 5.3 collective-permute-start.1
  220.5 3.6 collective-permute-start.2
  226.1 4.5 collective-permute-done.3
  238.1 72.8 %all-gather.2.cloned.1.call-done = f32[256,24,8,128]{3,2,1,0:T(8,128)} async-done(((f32[2,24,8,128]{3,2,1,0:T(8,128)}), f32[256,24,8,128]{3,2,1,0:T(8,128)}) %all-gather.2.cloned.1.call-update) | async-done | bytes 25165840 | tf_op jit(solution)/shard_map/all_gather | solution.py:135
  310.9 1715.0 %while.16 = (s32[]{:T(128)}, f32[24,80,384]{2,1,0:T(8,128)}, f32[256,24,8,128]{3,2,1,0:T(8,128)}, s32[16,2]{0,1:T(2,128)S(1)}, s32[]{:T(128)}, /*index=5*/s32[]{...) while((s32[]{:T(128)}, f32[24,80,384]{2,1,0:T(8,128)}, ...), condition=%wide.region_3.4_spmd, body=%wide.region_2.3_spmd.sunk | while | flops 46 | bytes 393896 | solution.py:150
  692.0 3.2 dynamic_update_slice.12
  698.1 8.7 dynamic_update_slice.12
  715.6 8.7 dynamic_update_slice.12
  733.2 8.7 dynamic_update_slice.12
  750.7 8.7 dynamic_update_slice.12
  768.3 8.7 dynamic_update_slice.12
  785.9 8.7 dynamic_update_slice.12
  803.4 8.7 dynamic_update_slice.12
  821.0 8.7 dynamic_update_slice.12
  838.5 8.7 dynamic_update_slice.12
  856.1 8.7 dynamic_update_slice.12
  873.6 8.7 dynamic_update_slice.12
  891.2 8.7 dynamic_update_slice.12
  908.7 8.7 dynamic_update_slice.12
  926.3 8.7 dynamic_update_slice.12
  943.9 8.7 dynamic_update_slice.12
  961.4 8.7 dynamic_update_slice.12
  1177.1 8.7 dynamic_update_slice.12
  1194.7 8.7 dynamic_update_slice.12
  1212.2 8.7 dynamic_update_slice.12
  1229.8 8.7 dynamic_update_slice.12
  1247.3 8.7 dynamic_update_slice.12
  1264.9 8.7 dynamic_update_slice.12
  1282.5 8.7 dynamic_update_slice.12
  1300.0 8.7 dynamic_update_slice.12
  1317.6 8.7 dynamic_update_slice.12
  1335.1 8.7 dynamic_update_slice.12
  1352.7 8.7 dynamic_update_slice.12
  1370.2 8.7 dynamic_update_slice.12
  1387.8 8.7 dynamic_update_slice.12
  1405.4 8.7 dynamic_update_slice.12
  1422.9 8.7 dynamic_update_slice.12
  1440.4 8.7 dynamic_update_slice.12
  1578.0 3.2 dynamic_update_slice.12
  1602.1 3.2 dynamic_update_slice.12
  1638.2 3.2 dynamic_update_slice.12
  1782.4 3.2 dynamic_update_slice.12
  1806.5 3.2 dynamic_update_slice.12
  (1088 shorter events, 1140.8 us)
Async XLA Ops:
  7.2 4.3 copy-start
  7.2 153.0 %all-reduce.3.cloned.1.call-start = ((), (), s32[]{:S(2)}) async-start(), calls=%async_computation | async-start | bytes 1572864 | tf_op jit(solution)/shard_map/psum | solution.py:102
  11.9 3.1 copy-start.4
  14.9 7.1 copy-start.7
  14.9 7.2 copy-start.6
  14.9 295.9 %all-gather.2.cloned.1.call-start = ((), (), s32[]{:S(2)}) async-start(), calls=%async_computation.1 | async-start | bytes 25362432 | tf_op jit(solution)/shard_map/all_gather | solution.py:135
  15.3 1.2 copy-start.3
  16.5 147.4 %collective-permute-start.4 = (f32[2,24,1,384]{3,1,2,0:T(8,128)S(1)}, f32[2,24,1,384]{3,1,2,0:T(8,128)S(1)}, u32[]{:S(2)}, u32[]{:S(2)}) collective-permute-start(f32[2,24,1,384]{3,1,2,0:T(8,128)S(1)} %get-tuple-element.229), channel_id=1, source_target_pairs={{0,1},{1,2},{2,3},{3,4},{4,5},{5,6},{6,7},{7,8},{8,9},{9,10},{10,1... | collective-permute-start | bytes 221192 | tf_op jit(solution)/shard_map/ppermute | solution.py:14
  19.8 144.1 %collective-permute-start.5 = (f32[2,24,1,384]{3,1,2,0:T(8,128)S(1)}, f32[2,24,1,384]{3,1,2,0:T(8,128)S(1)}, u32[]{:S(2)}, u32[]{:S(2)}) collective-permute-start(f32[2,24,1,384]{3,1,2,0:T(8,128)S(1)} %get-tuple-element.230), channel_id=1, source_target_pairs={{1,0},{2,1},{3,2},{4,3},{5,4},{6,5},{7,6},{8,7},{9,8},{10,9},{11,1... | collective-permute-start | bytes 221192 | tf_op jit(solution)/shard_map/ppermute | solution.py:15
  163.9 12.5 copy-start.1
  168.2 5.8 collective-permute-start.6
  171.0 5.1 collective-permute-start.7
  178.6 5.6 collective-permute-start.8
  180.5 5.9 copy-start.2
  180.6 5.5 collective-permute-start.9
  210.0 6.6 collective-permute-start
  211.3 6.1 collective-permute-start.1
  220.5 10.5 collective-permute-start.2
  224.2 6.4 collective-permute-start.3
  236.5 74.3 %copy-start.5 = (s32[16,2]{0,1:T(2,128)S(1)}, s32[16,2]{0,1:T(2,128)}, u32[]{:S(2)}) copy-start(s32[16,2]{0,1:T(2,128)} %param.9) | copy-start | bytes 388
Sparse Core Ops, SparseCore 0:
  15.0 145.1 all-reduce.2
  210.1 100.7 all-gather.1
where the time goes:
time: 2070 us; the launch traced here: 2030 us
  local copies, waits for them, and re-layouts  1410 us (68%)
  loops' own time  332 us (16%)
  waiting for transfers between devices  221 us (11%)
  starting transfers between devices  28.4 us (1%)
  other arithmetic  24.7 us (1%)
    dynamic_update_slice x256, local copies, waits for them, and re-layouts, put_one(): lax.dynamic_update_slice(canvas_inner, piece, (zero_start, top_at, left_at))  985 us
    another operation x1, loops' own time, shards(): filled = lax.fori_loop(0, item_count, put_one, canvas)  332 us
    squeeze x256, local copies, waits for them, and re-layouts, put_one(): piece = lax.dynamic_index_in_dim(pieces, item, 0, keepdims=False)  232 us
    slice x256, local copies, waits for them, and re-layouts, put_one(): anchor[0, 1] - col_base + foot_cols  148 us
    psum x1, waiting for transfers between devices, shards(): cycle_every = lax.psum(contrib, ('grp', 'dev'))  138 us
    all_gather x1, waiting for transfers between devices, shards(): pieces = lax.all_gather(averages, ('grp', 'dev'), axis=0, tiled=True)  72.8 us
  transfers between devices with their start and end apart: 12, of which 7 were waited for; matrix products, arithmetic and copies ran while one was open for 1% of the time, Pallas kernels for 0%

commit v1 on v0

v1 whole, which is shorter than its diff:
```python
import functools

import jax
import jax.numpy as jnp
from jax import lax
from jax.experimental import pallas as pl
from jax.experimental.pallas import tpu as pltpu
from jax.sharding import PartitionSpec as P

F32 = jnp.float32
BF16 = jnp.bfloat16
I32 = jnp.int32
MESH = pl.DeviceIdType.MESH

G = 8
D = 16
C = 24
CH = C // 2
TR = 64
TC = 128
NR = 24
NC = 384
FP = 128
BAND = 256
NESTS = 16
PLANES = 2 * C
WR = NR + 16
LEAD = 8


def iota(shape, axis):
    return lax.broadcasted_iota(I32, shape, axis)


def remote(src, dst, send, recv, axis, target):
    return pltpu.make_async_remote_copy(
        src_ref=src,
        dst_ref=dst,
        send_sem=send,
        recv_sem=recv,
        device_id={axis: target},
        device_id_type=MESH,
    )


def split3(a):
    hi = a.astype(BF16)
    rest = a - hi.astype(F32)
    mid = rest.astype(BF16)
    return hi, mid, (rest - mid.astype(F32)).astype(BF16)


def kernel(
    anchor,
    diff,
    cour,
    parent,
    nest,
    pout,
    nout,
    work,
    pv,
    prow_in,
    pcol,
    pcol_in,
    item,
    item_in,
    wecol,
    strip,
    strip_in,
    edge,
    edge_in,
    ghost,
    fine,
    colsum,
    avg,
    slabs,
    slab_out,
    canvas,
    half,
    half_in,
    adv,
    tab,
    local_sem,
    halo_sem,
    item_sem,
    strip_sem,
    edge_sem,
    slab_sem,
    canvas_sem,
    half_sem,
):
    g = lax.axis_index("grp")
    d = lax.axis_index("dev")
    core = g % 2
    row0 = g * TR
    col0 = d * TC
    lane = iota((1, 128), 1)

    own_nest = pltpu.make_async_copy(nest, work.at[:, pl.ds(8, NR), :], local_sem.at[0])
    own_nest.start()
    own_parent = pltpu.make_async_copy(parent, pv, local_sem.at[1])
    own_parent.start()

    barrier = pltpu.get_barrier_semaphore()
    for k in range(1, G):
        pl.semaphore_signal(barrier, inc=1, device_id={"grp": (g + k) % G}, device_id_type=MESH)
    for k in range(1, D):
        pl.semaphore_signal(barrier, inc=1, device_id={"dev": (d + k) % D}, device_id_type=MESH)

    key = [anchor[n, 0] // BAND * 8 + anchor[n, 1] // BAND for n in range(NESTS)]
    band_row = g // 4
    for b in range(8):
        found = jnp.int32(0)
        for n in range(NESTS):
            found = jnp.where(key[n] == band_row * 8 + b, n, found)
        tab[b] = found
    other = jnp.int32(0)
    for n in range(NESTS):
        other = jnp.where(key[n] == (1 - band_row) * 8 + d // 2, n, other)
    mine = tab[d // 2]
    odd = d % 2
    beside = tab[jnp.clip(d // 2 - 1 + 2 * odd, 0, 7)]

    r_m, q_m = anchor[mine, 0], anchor[mine, 1]
    west_m = q_m - 1 - col0
    east_m = q_m + FP - col0
    is_west = (west_m >= 0) & (west_m < TC)
    is_east = (east_m >= 0) & (east_m < TC)
    pick = jnp.where(is_west, west_m, jnp.where(is_east, east_m, 0))
    q_b = anchor[beside, 1]
    beside_on = jnp.where(odd == 1, q_b == col0 + TC, q_b + FP == col0)

    south_m = r_m - 1 - row0
    north_m = r_m + FP - row0
    is_south = (south_m >= 0) & (south_m < TR)
    is_north = (north_m >= 0) & (north_m < TR)
    row_pick = jnp.where(is_south, south_m, jnp.where(is_north, north_m, 0))
    r_o, q_o = anchor[other, 0], anchor[other, 1]
    low = band_row == 0
    other_on = jnp.where(low, r_o == row0 + TR, r_o + FP == row0)

    own_parent.wait()

    def gather(c, carry):
        first, last, picked, row_m, row_o = carry
        x = pv[c]
        here = lane == c
        first = jnp.where(here, pltpu.roll(x, c, 1), first)
        last = jnp.where(here, pltpu.roll(x, c + 1, 1), last)
        picked = jnp.where(here, pltpu.roll(x, (c - pick) & 127, 1), picked)
        sub = iota((C, 128), 0) == c
        row_m = jnp.where(sub, pv[c, pl.ds(row_pick, 1), :], row_m)
        edge_row = jnp.where(low, x[TR - 1 : TR], x[0:1])
        row_o = jnp.where(sub, edge_row, row_o)
        return first, last, picked, row_m, row_o

    zero_col = jnp.zeros((TR, 128), F32)
    zero_row = jnp.zeros((C, 128), F32)
    first, last, picked, row_m, row_o = lax.fori_loop(
        0, C, gather, (zero_col, zero_col, zero_col, zero_row, zero_row)
    )
    pcol[0] = first
    pcol[1] = last
    side = jnp.where(odd == 1, last, first)
    place_m = (mine % 2) * 48 + jnp.where(is_west, 0, C)
    place_b = (beside % 2) * 48 + jnp.where(odd == 1, 0, C)
    cols_m = pltpu.roll(picked, place_m, 1)
    cols_b = pltpu.roll(side, place_b, 1)
    span_m = lane + (q_m - col0)
    span_o = lane + (q_o - col0)
    rows_m = jnp.where((span_m >= 0) & (span_m < TC), pltpu.roll(row_m, (col0 - q_m) & 127, 1), 0.0)
    rows_o = jnp.where((span_o >= 0) & (span_o < TC), pltpu.roll(row_o, (col0 - q_o) & 127, 1), 0.0)
    for t in range(G):
        a_m = jnp.where((mine // 2 == t) & (is_west | is_east), 1, 0)
        a_b = jnp.where((beside // 2 == t) & beside_on, 1, 0)
        item[t, pl.ds(0, TR), :] = jnp.where(a_m == 1, cols_m, 0.0) + jnp.where(a_b == 1, cols_b, 0.0)
        for a in range(2):
            s_m = jnp.where((mine == 2 * t + a) & (is_south | is_north), 1, 0)
            s_o = jnp.where((other == 2 * t + a) & other_on, 1, 0)
            item[t, pl.ds(TR + C * a, C), :] = jnp.where(s_m == 1, rows_m, 0.0) + jnp.where(
                s_o == 1, rows_o, 0.0
            )

    pl.semaphore_wait(barrier, G + D - 2)

    sends = []
    for k in range(1, G):
        t = (g + k) % G
        cp = remote(item.at[t], item_in.at[g], item_sem.at[0, k], item_sem.at[1, k], "grp", t)
        cp.start()
        sends.append(cp)
    up_g, dn_g = (g + 1) % G, (g + G - 1) % G
    up_d, dn_d = (d + 1) % D, (d + D - 1) % D
    halos = [
        remote(parent.at[:, pl.ds(TR - 1, 1), :], prow_in.at[0, :, pl.ds(0, 1), :], halo_sem.at[0, 0], halo_sem.at[1, 0], "grp", up_g),
        remote(parent.at[:, pl.ds(0, 1), :], prow_in.at[1, :, pl.ds(0, 1), :], halo_sem.at[0, 1], halo_sem.at[1, 1], "grp", dn_g),
        remote(pcol.at[1], pcol_in.at[0], halo_sem.at[0, 2], halo_sem.at[1, 2], "dev", up_d),
        remote(pcol.at[0], pcol_in.at[1], halo_sem.at[0, 3], halo_sem.at[1, 3], "dev", dn_d),
        remote(nest.at[:, pl.ds(NR - 3, 3), :], work.at[:, pl.ds(5, 3), :], halo_sem.at[0, 4], halo_sem.at[1, 4], "dev", up_d),
        remote(nest.at[:, pl.ds(0, 3), :], work.at[:, pl.ds(8 + NR, 3), :], halo_sem.at[0, 5], halo_sem.at[1, 5], "dev", dn_d),
    ]
    for cp in halos:
        cp.start()

    item_in[g] = item[g]

    for k in range(1, G):
        s = (g + G - k) % G
        remote(item.at[s], item_in.at[s], item_sem.at[0, k], item_sem.at[1, k], "grp", s).wait_recv()
    wecol[pl.ds(0, LEAD), :] = jnp.zeros((LEAD, 128), F32)
    wecol[pl.ds(LEAD + G * TR, 32), :] = jnp.zeros((32, 128), F32)
    south = [jnp.zeros((C, 128), F32)] * 2
    north = [jnp.zeros((C, 128), F32)] * 2
    r_own = [anchor[2 * g + a, 0] for a in range(2)]
    for s in range(G):
        wecol[pl.ds(LEAD + s * TR, TR), :] = item_in[s, pl.ds(0, TR), :]
        for a in range(2):
            got = item_in[s, pl.ds(TR + C * a, C), :]
            below = r_own[a] - 1 - s * TR
            above = r_own[a] + FP - s * TR
            south[a] = south[a] + jnp.where((below >= 0) & (below < TR), got, 0.0)
            north[a] = north[a] + jnp.where((above >= 0) & (above < TR), got, 0.0)
    for a in range(2):
        edge[0, pl.ds(C * a, C), :] = south[a]
        edge[1, pl.ds(C * a, C), :] = north[a]

    def strip_of(t):
        parts = [wecol[pl.ds(LEAD - 1 + r_own[a] + 8 * t, 16), :] for a in range(2)]
        return jnp.where(lane < 48, parts[0], parts[1])

    for k in range(1, D):
        t = (d + k) % D
        strip[k] = strip_of(t)
        cp = remote(strip.at[k], strip_in.at[k], strip_sem.at[0, k], strip_sem.at[1, k], "dev", t)
        cp.start()
        sends.append(cp)
    strip_in[0] = strip_of(d)

    for e, end in ((0, 0), (1, D - 1)):

        @pl.when(d != end)
        def _(e=e, end=end):
            remote(edge.at[e], edge_in.at[d], edge_sem.at[0, e], edge_sem.at[1, d], "dev", end).start()

    for cp in halos[:4]:
        cp.wait()
    tile = iota((TR, 128), 0)

    def parent_step(c, _):
        mid = pv[c]
        kx, ky = diff[0, c], diff[1, c]
        ax, ay = cour[0, c], cour[1, c]
        gw = jnp.where(d == 0, 0.0, pltpu.roll(pcol_in[0], (128 - c) & 127, 1))
        ge = jnp.where(d == D - 1, 0.0, pltpu.roll(pcol_in[1], 127 - c, 1))
        gs = jnp.where(g == 0, 0.0, prow_in[0, c, 0:1, :])
        gn = jnp.where(g == G - 1, 0.0, prow_in[1, c, 0:1, :])
        west = jnp.where(lane == 0, gw, pltpu.roll(mid, 1, 1))
        east = jnp.where(lane == 127, ge, pltpu.roll(mid, 127, 1))
        below = jnp.where(tile == 0, gs, pltpu.roll(mid, 1, 0))
        above = jnp.where(tile == TR - 1, gn, pltpu.roll(mid, TR - 1, 0))
        adv[c] = (
            mid * (1.0 - 2.0 * kx - 2.0 * ky - ax - ay)
            + kx * east
            + (kx + ax) * west
            + ky * above
            + (ky + ay) * below
        )
        return 0

    lax.fori_loop(0, C, parent_step, 0)

    for k in range(1, D):
        remote(strip.at[k], strip_in.at[k], strip_sem.at[0, k], strip_sem.at[1, k], "dev", d).wait_recv()
    total = strip_in[0]
    for k in range(1, D):
        total = total + strip_in[k]
    for i in range(10):
        ghost[pl.ds(5 + 3 * i, 3), :] = jnp.broadcast_to(total[i : i + 1], (3, 128))

    for e, end in ((0, 0), (1, D - 1)):

        @pl.when(d == end)
        def _(e=e, end=end):
            whole = edge[e]
            for k in range(1, D):
                s = (end + k) % D
                remote(edge.at[e], edge_in.at[s], edge_sem.at[0, e], edge_sem.at[1, s], "dev", end).wait_recv()
            for k in range(1, D):
                whole = whole + edge_in[(end + k) % D]
            off = iota((TC, NC), 1) - 3 * iota((TC, NC), 0)
            spread = jnp.where((off >= 0) & (off < 3), 1.0, 0.0).astype(BF16)
            spread_out = sum(
                jnp.dot(part, spread, preferred_element_type=F32) for part in split3(whole)
            )
            for j in range(3):
                fine[j] = spread_out[:, 128 * j : 128 * j + 128]

        @pl.when(d != end)
        def _(e=e, end=end):
            remote(edge.at[e], edge_in.at[d], edge_sem.at[0, e], edge_sem.at[1, d], "dev", end).wait_send()

    for cp in halos[4:]:
        cp.wait()
    own_nest.wait()

    off = iota((NC, TC), 0) - 3 * iota((NC, TC), 1)
    collect = jnp.where((off >= 0) & (off < 3), 1.0, 0.0).astype(BF16)
    fine_row = iota((WR, 128), 0)
    fixed = ((fine_row == 7) & (d == 0)) | ((fine_row == 8 + NR) & (d == D - 1))

    def nest_step(p, _):
        c = lax.rem(p, C)
        base = 48 * (p // C) + c
        kx, ky = 3.0 * diff[0, c], 3.0 * diff[1, c]
        ax, ay = cour[0, c], cour[1, c]
        k_c, k_w, k_s = 1.0 - 2.0 * kx - 2.0 * ky - ax - ay, kx + ax, ky + ay
        cols = ghost[...]
        gw = pltpu.roll(cols, lax.rem(128 - base, 128), 1)
        ge = pltpu.roll(cols, 127 - C - base, 1)
        x = [work[p, :, pl.ds(128 * j, 128)] for j in range(3)]
        held = [fine[j, pl.ds(p, 1), :] for j in range(3)]
        for step in range(3):
            x = [jnp.where(fixed, held[j], x[j]) for j in range(3)]
            right = [gw] + [pltpu.roll(v, 1, 1) for v in x]
            left = [pltpu.roll(v, 127, 1) for v in x] + [ge]
            x = [
                k_c * x[j]
                + kx * jnp.where(lane == 127, left[j + 1], left[j])
                + k_w * jnp.where(lane == 0, right[j], right[j + 1])
                + ky * pltpu.roll(x[j], WR - 1, 0)
                + k_s * pltpu.roll(x[j], 1, 0)
                for j in range(3)
            ]
        for j in range(3):
            work[p, pl.ds(8, NR), pl.ds(128 * j, 128)] = x[j][8 : 8 + NR]
        return 0

    lax.fori_loop(0, PLANES, nest_step, 0)
    done_nest = pltpu.make_async_copy(work.at[:, pl.ds(8, NR), :], nout, local_sem.at[0])
    done_nest.start()

    def sum_cols(b, _):
        x = jnp.concatenate([work[8 * b + i, pl.ds(8, NR), :] for i in range(8)], axis=0)
        hi = x.astype(BF16)
        lo = (x - hi.astype(F32)).astype(BF16)
        colsum[pl.ds(pl.multiple_of(b * 8 * NR, 8 * NR), 8 * NR), :] = jnp.dot(
            hi, collect, preferred_element_type=F32
        ) + jnp.dot(lo, collect, preferred_element_type=F32)
        return 0

    lax.fori_loop(0, PLANES // 8, sum_cols, 0)
    mean = sum(colsum[pl.ds(k, PLANES * 8, stride=3), :] for k in range(3)) * (1.0 / 9.0)
    avg[...] = mean.reshape(2, C, 8, 128)

    for k in range(1, G):
        t = (g + k) % G
        cp = remote(
            avg.at[:, pl.ds(CH * (t % 2), CH)],
            slabs.at[pl.ds(2 * g, 2)],
            slab_sem.at[0, k],
            slab_sem.at[1, k],
            "grp",
            t,
        )
        cp.start()
        sends.append(cp)
    slabs[pl.ds(2 * g, 2)] = avg[:, pl.ds(CH * core, CH)]
    for k in range(1, G):
        s = (g + G - k) % G
        remote(
            avg.at[:, pl.ds(0, CH)],
            slabs.at[pl.ds(2 * s, 2)],
            slab_sem.at[0, k],
            slab_sem.at[1, k],
            "grp",
            s,
        ).wait_recv()

    for k in range(1, D):
        t = (d + k) % D
        slab_out[k] = slabs[tab[t // 2]]
        cp = remote(
            slab_out.at[k],
            canvas.at[:, pl.ds(64 + 8 * d, 8), :],
            canvas_sem.at[0, k],
            canvas_sem.at[1, k],
            "dev",
            t,
        )
        cp.start()
        sends.append(cp)
    canvas[:, pl.ds(64 + 8 * d, 8), :] = slabs[mine]
    for k in range(1, D):
        s = (d + D - k) % D
        remote(
            slab_out.at[k],
            canvas.at[:, pl.ds(64 + 8 * s, 8), :],
            canvas_sem.at[0, k],
            canvas_sem.at[1, k],
            "dev",
            s,
        ).wait_recv()

    pair = g + 1 - 2 * core
    pair_row = jnp.clip(pair * TR - r_m, -TR, FP) + TR
    half[...] = canvas[:, pl.ds(pair_row, TR), :]
    swap = remote(half, half_in, half_sem.at[0], half_sem.at[1], "grp", pair)
    swap.start()

    own_row = jnp.clip(row0 - r_m, -TR, FP) + TR
    shift = (q_m - col0) & 127
    tile_row = iota((TR, 128), 0) + (row0 - r_m)
    tile_col = iota((TR, 128), 1) + (col0 - q_m)
    covered = (tile_row >= 0) & (tile_row < FP) & (tile_col >= 0) & (tile_col < FP)

    def put_own(j, _):
        c = CH * core + j
        pv[c] = jnp.where(covered, pltpu.roll(canvas[j, pl.ds(own_row, TR), :], shift, 1), adv[c])
        return 0

    def put_other(j, _):
        c = CH * (1 - core) + j
        pv[c] = jnp.where(covered, pltpu.roll(half_in[j], shift, 1), adv[c])
        return 0

    lax.fori_loop(0, CH, put_own, 0)
    swap.wait()
    lax.fori_loop(0, CH, put_other, 0)
    done_parent = pltpu.make_async_copy(pv, pout, local_sem.at[1])
    done_parent.start()
    for cp in sends:
        cp.wait_send()
    done_nest.wait()
    done_parent.wait()


def shards(parent, nest, anchor, diffusion, courant):
    any_space = pl.BlockSpec(memory_space=pl.ANY)
    scalars = pl.BlockSpec(memory_space=pltpu.SMEM)
    dma = pltpu.SemaphoreType.DMA
    vmem = pltpu.VMEM
    pout, nout = pl.pallas_call(
        kernel,
        out_shape=(
            jax.ShapeDtypeStruct((C, TR, TC), F32),
            jax.ShapeDtypeStruct((PLANES, NR, NC), F32),
        ),
        in_specs=[scalars, scalars, scalars, any_space, any_space],
        out_specs=(any_space, any_space),
        scratch_shapes=[
            vmem((PLANES, WR, NC), F32),
            vmem((C, TR, TC), F32),
            vmem((2, C, 8, TC), F32),
            vmem((2, TR, 128), F32),
            vmem((2, TR, 128), F32),
            vmem((G, TR + PLANES, 128), F32),
            vmem((G, TR + PLANES, 128), F32),
            vmem((LEAD + G * TR + 32, 128), F32),
            vmem((D, 16, 128), F32),
            vmem((D, 16, 128), F32),
            vmem((2, PLANES, 128), F32),
            vmem((D, PLANES, 128), F32),
            vmem((WR, 128), F32),
            vmem((3, PLANES, 128), F32),
            vmem((PLANES * NR, TC), F32),
            vmem((2, C, 8, TC), F32),
            vmem((NESTS, CH, 8, TC), F32),
            vmem((D, CH, 8, TC), F32),
            vmem((CH, 256, TC), F32),
            vmem((CH, TR, TC), F32),
            vmem((CH, TR, TC), F32),
            vmem((C, TR, TC), F32),
            pltpu.SMEM((8,), I32),
            dma((2,)),
            dma((2, 6)),
            dma((2, G)),
            dma((2, D)),
            dma((2, D)),
            dma((2, G)),
            dma((2, D)),
            dma((2,)),
        ],
        compiler_params=pltpu.CompilerParams(
            collective_id=0, has_side_effects=True, vmem_limit_bytes=48 * 1024 * 1024
        ),
    )(anchor, diffusion, courant, parent, nest.reshape(PLANES, NR, NC))
    return pout, nout.reshape(2, C, NR, NC)


def solution(mesh):
    placed = (P(None, "grp", "dev"), P("grp", None, "dev", None), P(), P(), P())
    return jax.shard_map(
        shards,
        mesh=mesh,
        in_specs=placed,
        out_specs=(P(None, "grp", "dev"), P("grp", None, "dev", None)),
        check_vma=False,
    )
```

time: 2070 us -> 69.4 us (0.03)
  the two profiles are of different devices: /device:TPU:95 before, /device:TPU:1 now
where the time goes in v1:
time: 69.4 us; the launch traced here: 69 us
  Pallas kernels  61.6 us (89%)
  local copies, waits for them, and re-layouts  6.81 us (10%)
    pallas_call x1, Pallas kernels, shards(): pl.pallas_call(kernel, out_shape=(jax.ShapeDtypeStruct((C, TR, TC), F32),...  61.6 us
    unnamed x11, local copies, waits for them, and re-layouts  6.81 us

profile of v1, /device:TPU:1, one launch (start us, length us, event | category | flops | bytes accessed | tf_op | source)
XLA Modules:
  0.0 69.0 jit_solution(15878595529884810069)
XLA Ops:
  0.6 0.8 %copy.7.anchor = s32[16,2]{1,0:T(8,128)S(1)} copy(s32[16,2]{0,1:T(2,128)} %param.7) | data formatting | bytes 256 | tf_op args[2]
  1.4 0.0 copy-start
  1.4 1.5 %copy-done = f32[2,24,24,384]{3,2,1,0:T(8,128)S(1)} copy-done((f32[2,24,24,384]{3,2,1,0:T(8,128)S(1)}, f32[2,24,24,384]{3,2,1,0:T(8,128)}, u32[]{:S(2)}) %copy-start) | copy-done | bytes 1769496
  2.9 0.0 copy-start.1
  2.9 1.1 %copy-done.1 = f32[24,64,128]{2,1,0:T(8,128)S(1)} copy-done((f32[24,64,128]{2,1,0:T(8,128)S(1)}, f32[24,64,128]{2,1,0:T(8,128)}, u32[]{:S(2)}) %copy-start.1) | copy-done | bytes 786456
  4.0 0.0 copy-start.2
  4.0 0.7 copy-done.2
  4.7 0.0 copy-start.3
  4.7 0.7 copy-done.3
  5.4 61.6 %shard_map.68 = (f32[24,64,128]{2,1,0:T(8,128)S(1)}, f32[48,24,384]{2,1,0:T(8,128)S(1)}) custom-call(s32[16,2]{1,0:T(8,128)S(1)} %copy.7.anchor, f32[2,24]{1,0:T(2,128)S(1)} %copy-done.2, f32[2,24]{1,0:T(2,128)S(1)} %copy-done.3, f32[24,64,128]{2,1,0:T(8,128)S(1)} %copy-done.1, f32[48,24,384]{2,1,0:T(8,128)S(1)} %bitcast.3), custom_call_target="tpu_custom_call" | custom-call | tf_op jit(solution)/shard_map/pallas_call | solution.py:443
  66.9 0.9 %copy.10 = f32[24,64,128]{2,1,0:T(8,128)} copy(f32[24,64,128]{2,1,0:T(8,128)S(1)} %get-tuple-element.8) | data formatting | bytes 1572864
  67.8 1.2 %copy.11 = f32[2,24,24,384]{3,2,1,0:T(8,128)} copy(f32[2,24,24,384]{3,2,1,0:T(8,128)S(1)} %bitcast.2) | data formatting | bytes 3538944
Async XLA Ops:
  1.4 1.5 %copy-start = (f32[2,24,24,384]{3,2,1,0:T(8,128)S(1)}, f32[2,24,24,384]{3,2,1,0:T(8,128)}, u32[]{:S(2)}) copy-start(f32[2,24,24,384]{3,2,1,0:T(8,128)} %param.6) | copy-start | bytes 5308420
  2.9 1.1 %copy-start.1 = (f32[24,64,128]{2,1,0:T(8,128)S(1)}, f32[24,64,128]{2,1,0:T(8,128)}, u32[]{:S(2)}) copy-start(f32[24,64,128]{2,1,0:T(8,128)} %parent.1) | copy-start | bytes 2359300
  4.0 0.7 copy-start.2
  4.7 0.7 copy-start.3

commit v2 on v1

--- a/solution.py
+++ b/solution.py
@@ -15,7 +15,6 @@
 G = 8
 D = 16
 C = 24
-CH = C // 2
 TR = 64
 TC = 128
 NR = 24
@@ -24,7 +23,6 @@
 BAND = 256
 NESTS = 16
 PLANES = 2 * C
-WR = NR + 16
 LEAD = 8
 
 
@@ -59,6 +57,7 @@
     pout,
     nout,
     work,
+    res,
     pv,
     prow_in,
     pcol,
@@ -72,15 +71,20 @@
     edge_in,
     ghost,
     fine,
-    colsum,
+    coef,
+    triple,
     avg,
-    slabs,
+    slabs0,
+    slabs1,
+    slabs2,
     slab_out,
-    canvas,
-    half,
-    half_in,
+    canvas0,
+    canvas1,
+    canvas2,
+    window,
     adv,
     tab,
+    row_sem,
     local_sem,
     halo_sem,
     item_sem,
@@ -88,8 +92,10 @@
     edge_sem,
     slab_sem,
     canvas_sem,
-    half_sem,
+    pair_sem,
 ):
+    slabs = (slabs0, slabs1, slabs2)
+    canvas = (canvas0, canvas1, canvas2)
     g = lax.axis_index("grp")
     d = lax.axis_index("dev")
     core = g % 2
@@ -97,10 +103,11 @@
     col0 = d * TC
     lane = iota((1, 128), 1)
 
-    own_nest = pltpu.make_async_copy(nest, work.at[:, pl.ds(8, NR), :], local_sem.at[0])
-    own_nest.start()
-    own_parent = pltpu.make_async_copy(parent, pv, local_sem.at[1])
+    own_parent = pltpu.make_async_copy(parent, pv, local_sem.at[0])
     own_parent.start()
+    own_nest = [pltpu.make_async_copy(nest.at[:, r, :], work.at[3 + r], row_sem.at[r]) for r in range(NR)]
+    for cp in own_nest:
+        cp.start()
 
     barrier = pltpu.get_barrier_semaphore()
     for k in range(1, G):
@@ -139,6 +146,12 @@
     r_o, q_o = anchor[other, 0], anchor[other, 1]
     low = band_row == 0
     other_on = jnp.where(low, r_o == row0 + TR, r_o + FP == row0)
+
+    for c in range(C):
+        kx, ky = 3.0 * diff[0, c], 3.0 * diff[1, c]
+        ax, ay = cour[0, c], cour[1, c]
+        for i, v in enumerate((1.0 - 2.0 * kx - 2.0 * ky - ax - ay, kx, kx + ax, ky, ky + ay)):
+            coef[i, pl.ds(c, 1), :] = jnp.full((1, 128), v, F32)
 
     own_parent.wait()
 
@@ -197,10 +210,14 @@
         remote(parent.at[:, pl.ds(0, 1), :], prow_in.at[1, :, pl.ds(0, 1), :], halo_sem.at[0, 1], halo_sem.at[1, 1], "grp", dn_g),
         remote(pcol.at[1], pcol_in.at[0], halo_sem.at[0, 2], halo_sem.at[1, 2], "dev", up_d),
         remote(pcol.at[0], pcol_in.at[1], halo_sem.at[0, 3], halo_sem.at[1, 3], "dev", dn_d),
-        remote(nest.at[:, pl.ds(NR - 3, 3), :], work.at[:, pl.ds(5, 3), :], halo_sem.at[0, 4], halo_sem.at[1, 4], "dev", up_d),
-        remote(nest.at[:, pl.ds(0, 3), :], work.at[:, pl.ds(8 + NR, 3), :], halo_sem.at[0, 5], halo_sem.at[1, 5], "dev", dn_d),
+        remote(work.at[pl.ds(NR, 3)], work.at[pl.ds(0, 3)], halo_sem.at[0, 4], halo_sem.at[1, 4], "dev", up_d),
+        remote(work.at[pl.ds(3, 3)], work.at[pl.ds(NR + 3, 3)], halo_sem.at[0, 5], halo_sem.at[1, 5], "dev", dn_d),
     ]
-    for cp in halos:
+    for cp in halos[:4]:
+        cp.start()
+    for cp in own_nest:
+        cp.wait()
+    for cp in halos[4:]:
         cp.start()
 
     item_in[g] = item[g]
@@ -275,8 +292,7 @@
     total = strip_in[0]
     for k in range(1, D):
         total = total + strip_in[k]
-    for i in range(10):
-        ghost[pl.ds(5 + 3 * i, 3), :] = jnp.broadcast_to(total[i : i + 1], (3, 128))
+    ghost[...] = jnp.transpose(jnp.concatenate([total, jnp.zeros((112, 128), F32)], axis=0))
 
     for e, end in ((0, 0), (1, D - 1)):
 
@@ -290,11 +306,9 @@
                 whole = whole + edge_in[(end + k) % D]
             off = iota((TC, NC), 1) - 3 * iota((TC, NC), 0)
             spread = jnp.where((off >= 0) & (off < 3), 1.0, 0.0).astype(BF16)
-            spread_out = sum(
+            fine[...] = sum(
                 jnp.dot(part, spread, preferred_element_type=F32) for part in split3(whole)
             )
-            for j in range(3):
-                fine[j] = spread_out[:, 128 * j : 128 * j + 128]
 
         @pl.when(d != end)
         def _(e=e, end=end):
@@ -302,137 +316,165 @@
 
     for cp in halos[4:]:
         cp.wait()
-    own_nest.wait()
 
     off = iota((NC, TC), 0) - 3 * iota((NC, TC), 1)
     collect = jnp.where((off >= 0) & (off < 3), 1.0, 0.0).astype(BF16)
-    fine_row = iota((WR, 128), 0)
-    fixed = ((fine_row == 7) & (d == 0)) | ((fine_row == 8 + NR) & (d == D - 1))
-
-    def nest_step(p, _):
-        c = lax.rem(p, C)
-        base = 48 * (p // C) + c
-        kx, ky = 3.0 * diff[0, c], 3.0 * diff[1, c]
-        ax, ay = cour[0, c], cour[1, c]
-        k_c, k_w, k_s = 1.0 - 2.0 * kx - 2.0 * ky - ax - ay, kx + ax, ky + ay
-        cols = ghost[...]
-        gw = pltpu.roll(cols, lax.rem(128 - base, 128), 1)
-        ge = pltpu.roll(cols, 127 - C - base, 1)
-        x = [work[p, :, pl.ds(128 * j, 128)] for j in range(3)]
-        held = [fine[j, pl.ds(p, 1), :] for j in range(3)]
-        for step in range(3):
-            x = [jnp.where(fixed, held[j], x[j]) for j in range(3)]
-            right = [gw] + [pltpu.roll(v, 1, 1) for v in x]
-            left = [pltpu.roll(v, 127, 1) for v in x] + [ge]
-            x = [
-                k_c * x[j]
-                + kx * jnp.where(lane == 127, left[j + 1], left[j])
-                + k_w * jnp.where(lane == 0, right[j], right[j + 1])
-                + ky * pltpu.roll(x[j], WR - 1, 0)
-                + k_s * pltpu.roll(x[j], 1, 0)
-                for j in range(3)
+    first_dev, last_dev = d == 0, d == D - 1
+    tiles = range(3)
+
+    def substeps(j, a):
+        plane = pl.ds(pl.multiple_of(C * a + 8 * j, 8), 8)
+        k_c, k_x, k_w, k_y, k_s = (coef[i, pl.ds(8 * j, 8), :] for i in range(5))
+        west = ghost[pl.ds(pl.multiple_of(48 * a + 8 * j, 8), 8), :]
+        east = ghost[pl.ds(pl.multiple_of(48 * a + C + 8 * j, 8), 8), :]
+        held = [fine[plane, pl.ds(128 * i, 128)] for i in tiles]
+        sides = {}
+
+        def ghosts(w):
+            i = w // 3
+            if i not in sides:
+                sides[i] = (pltpu.roll(west, (128 - i) % 128, 1), pltpu.roll(east, 127 - i, 1))
+            return sides[i]
+
+        def keep(w, row):
+            if w == 2:
+                return [jnp.where(first_dev, held[i], row[i]) for i in tiles]
+            if w == NR + 3:
+                return [jnp.where(last_dev, held[i], row[i]) for i in tiles]
+            return row
+
+        def advance(w, below, row, above):
+            gw, ge = ghosts(w)
+            right = [gw] + [pltpu.roll(v, 1, 1) for v in row]
+            left = [pltpu.roll(v, 127, 1) for v in row] + [ge]
+            return [
+                k_c * row[i]
+                + k_x * jnp.where(lane == 127, left[i + 1], left[i])
+                + k_w * jnp.where(lane == 0, right[i], right[i + 1])
+                + k_y * above[i]
+                + k_s * below[i]
+                for i in tiles
             ]
-        for j in range(3):
-            work[p, pl.ds(8, NR), pl.ds(128 * j, 128)] = x[j][8 : 8 + NR]
-        return 0
-
-    lax.fori_loop(0, PLANES, nest_step, 0)
-    done_nest = pltpu.make_async_copy(work.at[:, pl.ds(8, NR), :], nout, local_sem.at[0])
-    done_nest.start()
-
-    def sum_cols(b, _):
-        x = jnp.concatenate([work[8 * b + i, pl.ds(8, NR), :] for i in range(8)], axis=0)
-        hi = x.astype(BF16)
-        lo = (x - hi.astype(F32)).astype(BF16)
-        colsum[pl.ds(pl.multiple_of(b * 8 * NR, 8 * NR), 8 * NR), :] = jnp.dot(
-            hi, collect, preferred_element_type=F32
-        ) + jnp.dot(lo, collect, preferred_element_type=F32)
-        return 0
-
-    lax.fori_loop(0, PLANES // 8, sum_cols, 0)
-    mean = sum(colsum[pl.ds(k, PLANES * 8, stride=3), :] for k in range(3)) * (1.0 / 9.0)
-    avg[...] = mean.reshape(2, C, 8, 128)
-
-    for k in range(1, G):
-        t = (g + k) % G
-        cp = remote(
-            avg.at[:, pl.ds(CH * (t % 2), CH)],
-            slabs.at[pl.ds(2 * g, 2)],
-            slab_sem.at[0, k],
-            slab_sem.at[1, k],
+
+        levels = [{}, {}, {}]
+        acc = None
+        for w in range(NR + 6):
+            levels[0][w] = keep(w, [work[w, plane, pl.ds(128 * i, 128)] for i in tiles])
+            for n in range(3):
+                v = w - n - 1
+                if v <= n or v >= NR + 5 - n:
+                    continue
+                src = levels[n]
+                made = advance(v, src[v - 1], src[v], src[v + 1])
+                del src[v - 1]
+                if n < 2:
+                    levels[n + 1][v] = keep(v, made)
+                    continue
+                for i in tiles:
+                    res[v - 3, plane, pl.ds(128 * i, 128)] = made[i]
+                acc = made if (v - 3) % 3 == 0 else [x + y for x, y in zip(acc, made)]
+                if (v - 3) % 3 == 2:
+                    at = pl.ds(pl.multiple_of(64 * a + 8 * ((v - 3) // 3), 8), 8)
+                    for i in tiles:
+                        triple[at, pl.ds(128 * i, 128)] = acc[i]
+
+    pair = g + 1 - 2 * core
+
+    def slab_copy(j, k, t, mine_g):
+        return remote(
+            avg.at[j, :, pl.ds(4 * (t % 2), 4)],
+            slabs[j].at[pl.ds(2 * mine_g, 2)],
+            slab_sem.at[0, j, k],
+            slab_sem.at[1, j, k],
             "grp",
             t,
         )
-        cp.start()
-        sends.append(cp)
-    slabs[pl.ds(2 * g, 2)] = avg[:, pl.ds(CH * core, CH)]
-    for k in range(1, G):
-        s = (g + G - k) % G
-        remote(
-            avg.at[:, pl.ds(0, CH)],
-            slabs.at[pl.ds(2 * s, 2)],
-            slab_sem.at[0, k],
-            slab_sem.at[1, k],
-            "grp",
-            s,
-        ).wait_recv()
-
-    for k in range(1, D):
-        t = (d + k) % D
-        slab_out[k] = slabs[tab[t // 2]]
-        cp = remote(
-            slab_out.at[k],
-            canvas.at[:, pl.ds(64 + 8 * d, 8), :],
-            canvas_sem.at[0, k],
-            canvas_sem.at[1, k],
+
+    def canvas_copy(j, k, t, mine_d):
+        return remote(
+            slab_out.at[j, k],
+            canvas[j].at[8 + mine_d, core],
+            canvas_sem.at[0, j, k],
+            canvas_sem.at[1, j, k],
             "dev",
             t,
         )
+
+    def pair_copy(j, half):
+        block = canvas[j].at[pl.ds(8, D), half]
+        return remote(block, block, pair_sem.at[0, j], pair_sem.at[1, j], "grp", pair)
+
+    def to_groups(j):
+        for k in range(1, G):
+            cp = slab_copy(j, k, (g + k) % G, g)
+            cp.start()
+            sends.append(cp)
+        slabs[j][pl.ds(2 * g, 2)] = avg[j, :, pl.ds(4 * core, 4)]
+
+    def to_columns(j):
+        for k in range(1, G):
+            slab_copy(j, k, g, (g + G - k) % G).wait_recv()
+        for k in range(1, D):
+            t = (d + k) % D
+            slab_out[j, k] = slabs[j][tab[t // 2]]
+            cp = canvas_copy(j, k, t, d)
+            cp.start()
+            sends.append(cp)
+        canvas[j][8 + d, core] = slabs[j][mine]
+
+    def to_pair(j):
+        for k in range(1, D):
+            canvas_copy(j, k, d, (d + D - k) % D).wait_recv()
+        cp = pair_copy(j, core)
         cp.start()
         sends.append(cp)
-    canvas[:, pl.ds(64 + 8 * d, 8), :] = slabs[mine]
-    for k in range(1, D):
-        s = (d + D - k) % D
-        remote(
-            slab_out.at[k],
-            canvas.at[:, pl.ds(64 + 8 * s, 8), :],
-            canvas_sem.at[0, k],
-            canvas_sem.at[1, k],
-            "dev",
-            s,
-        ).wait_recv()
-
-    pair = g + 1 - 2 * core
-    pair_row = jnp.clip(pair * TR - r_m, -TR, FP) + TR
-    half[...] = canvas[:, pl.ds(pair_row, TR), :]
-    swap = remote(half, half_in, half_sem.at[0], half_sem.at[1], "grp", pair)
-    swap.start()
 
     own_row = jnp.clip(row0 - r_m, -TR, FP) + TR
     shift = (q_m - col0) & 127
     tile_row = iota((TR, 128), 0) + (row0 - r_m)
     tile_col = iota((TR, 128), 1) + (col0 - q_m)
     covered = (tile_row >= 0) & (tile_row < FP) & (tile_col >= 0) & (tile_col < FP)
-
-    def put_own(j, _):
-        c = CH * core + j
-        pv[c] = jnp.where(covered, pltpu.roll(canvas[j, pl.ds(own_row, TR), :], shift, 1), adv[c])
-        return 0
-
-    def put_other(j, _):
-        c = CH * (1 - core) + j
-        pv[c] = jnp.where(covered, pltpu.roll(half_in[j], shift, 1), adv[c])
-        return 0
-
-    lax.fori_loop(0, CH, put_own, 0)
-    swap.wait()
-    lax.fori_loop(0, CH, put_other, 0)
-    done_parent = pltpu.make_async_copy(pv, pout, local_sem.at[1])
-    done_parent.start()
+    rows_of = [c.reshape(256, 8, TC) for c in canvas]
+    outs = []
+
+    def place(j):
+        pair_copy(j, 1 - core).wait_recv()
+        window[...] = rows_of[j][pl.ds(own_row, TR)].reshape(8 * TR, TC)
+        for i in range(8):
+            c = 8 * j + i
+            under = pltpu.roll(window[pl.ds(i, TR, stride=8), :], shift, 1)
+            adv[c] = jnp.where(covered, under, adv[c])
+        cp = pltpu.make_async_copy(adv.at[pl.ds(8 * j, 8)], pout.at[pl.ds(8 * j, 8)], local_sem.at[1 + j])
+        cp.start()
+        outs.append(cp)
+
+    for j in range(3):
+
+        def one(a, _, j=j):
+            substeps(j, a)
+            return 0
+
+        lax.fori_loop(0, 2, one, 0)
+        x = triple[...]
+        hi = x.astype(BF16)
+        lo = (x - hi.astype(F32)).astype(BF16)
+        mean = jnp.dot(hi, collect, preferred_element_type=F32) + jnp.dot(lo, collect, preferred_element_type=F32)
+        avg[j] = (mean * (1.0 / 9.0)).reshape(2, 8, 8, TC)
+        to_groups(j)
+    for r in range(NR):
+        cp = pltpu.make_async_copy(res.at[r], nout.at[:, r, :], row_sem.at[r])
+        cp.start()
+        outs.append(cp)
+    for j in range(3):
+        to_columns(j)
+    for j in range(3):
+        to_pair(j)
+    for j in range(3):
+        place(j)
     for cp in sends:
         cp.wait_send()
-    done_nest.wait()
-    done_parent.wait()
+    for cp in outs:
+        cp.wait()
 
 
 def shards(parent, nest, anchor, diffusion, courant):
@@ -446,10 +488,11 @@
             jax.ShapeDtypeStruct((C, TR, TC), F32),
             jax.ShapeDtypeStruct((PLANES, NR, NC), F32),
         ),
-        in_specs=[scalars, scalars, scalars, any_space, any_space],
+        in_specs=[scalars] * 3 + [any_space] * 2,
         out_specs=(any_space, any_space),
         scratch_shapes=[
-            vmem((PLANES, WR, NC), F32),
+            vmem((NR + 6, PLANES, NC), F32),
+            vmem((NR, PLANES, NC), F32),
             vmem((C, TR, TC), F32),
             vmem((2, C, 8, TC), F32),
             vmem((2, TR, 128), F32),
@@ -461,25 +504,26 @@
             vmem((D, 16, 128), F32),
             vmem((2, PLANES, 128), F32),
             vmem((D, PLANES, 128), F32),
-            vmem((WR, 128), F32),
-            vmem((3, PLANES, 128), F32),
-            vmem((PLANES * NR, TC), F32),
-            vmem((2, C, 8, TC), F32),
-            vmem((NESTS, CH, 8, TC), F32),
-            vmem((D, CH, 8, TC), F32),
-            vmem((CH, 256, TC), F32),
-            vmem((CH, TR, TC), F32),
-            vmem((CH, TR, TC), F32),
+            vmem((128, 128), F32),
+            vmem((PLANES, NC), F32),
+            vmem((5, C, 128), F32),
+            vmem((128, NC), F32),
+            vmem((3, 2, 8, 8, TC), F32),
+            *[vmem((NESTS, 4, 8, TC), F32)] * 3,
+            vmem((3, D, 4, 8, TC), F32),
+            *[vmem((32, 2, 4, 8, TC), F32)] * 3,
+            vmem((8 * TR, TC), F32),
             vmem((C, TR, TC), F32),
             pltpu.SMEM((8,), I32),
-            dma((2,)),
+            dma((NR,)),
+            dma((4,)),
             dma((2, 6)),
             dma((2, G)),
             dma((2, D)),
             dma((2, D)),
-            dma((2, G)),
-            dma((2, D)),
-            dma((2,)),
+            dma((2, 3, G)),
+            dma((2, 3, D)),
+            dma((2, 3)),
         ],
         compiler_params=pltpu.CompilerParams(
             collective_id=0, has_side_effects=True, vmem_limit_bytes=48 * 1024 * 1024

time: 69.4 us -> 58 us (0.84)
  Pallas kernels: 61.6 us -> 50.3 us
    pallas_call x1, Pallas kernels: 61.6 us -> 50.3 us  [shards(): pl.pallas_call(kernel, out_shape=(jax.ShapeDtypeStruct((C, TR, TC), F32),...]
where the time goes in v2:
time: 58 us; the launch traced here: 57.8 us
  Pallas kernels  50.3 us (87%)
  local copies, waits for them, and re-layouts  6.81 us (12%)
  between operations  0.64 us (1%)
    pallas_call x1, Pallas kernels, shards(): pl.pallas_call(kernel, out_shape=(jax.ShapeDtypeStruct((C, TR, TC), F32),...  50.3 us
    unnamed x11, local copies, waits for them, and re-layouts  6.81 us

profile of v2, /device:TPU:1, one launch (start us, length us, event | category | flops | bytes accessed | tf_op | source)
XLA Modules:
  0.0 57.8 jit_solution(15627390367561484179)
XLA Ops:
  0.6 0.8 %copy.7.anchor = s32[16,2]{1,0:T(8,128)S(1)} copy(s32[16,2]{0,1:T(2,128)} %param.7) | data formatting | bytes 256 | tf_op args[2]
  1.4 0.0 copy-start
  1.4 1.5 %copy-done = f32[2,24,24,384]{3,2,1,0:T(8,128)S(1)} copy-done((f32[2,24,24,384]{3,2,1,0:T(8,128)S(1)}, f32[2,24,24,384]{3,2,1,0:T(8,128)}, u32[]{:S(2)}) %copy-start) | copy-done | bytes 1769496
  2.9 0.0 copy-start.1
  2.9 1.1 %copy-done.1 = f32[24,64,128]{2,1,0:T(8,128)S(1)} copy-done((f32[24,64,128]{2,1,0:T(8,128)S(1)}, f32[24,64,128]{2,1,0:T(8,128)}, u32[]{:S(2)}) %copy-start.1) | copy-done | bytes 786456
  4.0 0.0 copy-start.2
  4.0 0.7 %copy-done.2 = f32[2,24]{1,0:T(2,128)S(1)} copy-done((f32[2,24]{1,0:T(2,128)S(1)}, f32[2,24]{1,0:T(2,128)}, u32[]{:S(2)}) %copy-start.2) | copy-done | bytes 216
  4.7 0.0 copy-start.3
  4.7 0.7 %copy-done.3 = f32[2,24]{1,0:T(2,128)S(1)} copy-done((f32[2,24]{1,0:T(2,128)S(1)}, f32[2,24]{1,0:T(2,128)}, u32[]{:S(2)}) %copy-start.3) | copy-done | bytes 216
  5.4 50.3 %shard_map.68 = (f32[24,64,128]{2,1,0:T(8,128)S(1)}, f32[48,24,384]{2,1,0:T(8,128)S(1)}) custom-call(s32[16,2]{1,0:T(8,128)S(1)} %copy.7.anchor, f32[2,24]{1,0:T(2,128)S(1)} %copy-done.2, f32[2,24]{1,0:T(2,128)S(1)} %copy-done.3, f32[24,64,128]{2,1,0:T(8,128)S(1)} %copy-done.1, f32[48,24,384]{2,1,0:T(8,128)S(1)} %bitcast.3), custom_call_target="tpu_custom_call" | custom-call | tf_op jit(solution)/shard_map/pallas_call | solution.py:485
  55.7 0.9 %copy.10 = f32[24,64,128]{2,1,0:T(8,128)} copy(f32[24,64,128]{2,1,0:T(8,128)S(1)} %get-tuple-element.8) | data formatting | bytes 1572864
  56.5 1.2 %copy.11 = f32[2,24,24,384]{3,2,1,0:T(8,128)} copy(f32[2,24,24,384]{3,2,1,0:T(8,128)S(1)} %bitcast.2) | data formatting | bytes 3538944
Async XLA Ops:
  1.4 1.5 %copy-start = (f32[2,24,24,384]{3,2,1,0:T(8,128)S(1)}, f32[2,24,24,384]{3,2,1,0:T(8,128)}, u32[]{:S(2)}) copy-start(f32[2,24,24,384]{3,2,1,0:T(8,128)} %param.6) | copy-start | bytes 5308420
  2.9 1.1 %copy-start.1 = (f32[24,64,128]{2,1,0:T(8,128)S(1)}, f32[24,64,128]{2,1,0:T(8,128)}, u32[]{:S(2)}) copy-start(f32[24,64,128]{2,1,0:T(8,128)} %parent.1) | copy-start | bytes 2359300
  4.0 0.7 %copy-start.2 = (f32[2,24]{1,0:T(2,128)S(1)}, f32[2,24]{1,0:T(2,128)}, u32[]{:S(2)}) copy-start(f32[2,24]{1,0:T(2,128)} %diff.1) | copy-start | bytes 580
  4.7 0.7 %copy-start.3 = (f32[2,24]{1,0:T(2,128)S(1)}, f32[2,24]{1,0:T(2,128)}, u32[]{:S(2)}) copy-start(f32[2,24]{1,0:T(2,128)} %cour.1) | copy-start | bytes 580

commit v3 on v2

v3 whole, which is shorter than its diff:
```python
import functools

import jax
import jax.numpy as jnp
from jax import lax
from jax.experimental import pallas as pl
from jax.experimental.pallas import tpu as pltpu
from jax.sharding import PartitionSpec as P

F32 = jnp.float32
BF16 = jnp.bfloat16
I32 = jnp.int32
MESH = pl.DeviceIdType.MESH

G = 8
D = 16
C = 24
TR = 64
TC = 128
NR = 24
NC = 384
FP = 128
BAND = 256
NESTS = 16
PLANES = 2 * C
LEAD = 8


def iota(shape, axis):
    return lax.broadcasted_iota(I32, shape, axis)


def remote(src, dst, send, recv, axis, target):
    return pltpu.make_async_remote_copy(
        src_ref=src,
        dst_ref=dst,
        send_sem=send,
        recv_sem=recv,
        device_id={axis: target},
        device_id_type=MESH,
    )


def split3(a):
    hi = a.astype(BF16)
    rest = a - hi.astype(F32)
    mid = rest.astype(BF16)
    return hi, mid, (rest - mid.astype(F32)).astype(BF16)


def response(g, near, far, along):
    push = near * g
    a1 = along(None, push)
    b1 = along(a1, push)
    b2 = along(None, near * a1)
    c1 = along(b1, push + far * b2)
    c2 = along(b2, near * b1)
    c3 = along(None, near * b2)
    return c1, c2, c3


def select_dot(parts, matrix):
    return sum(jnp.dot(part, matrix, preferred_element_type=F32) for part in parts)


def one_hot(mask):
    return jnp.where(mask, 1.0, 0.0).astype(BF16)


def split2(a):
    hi = a.astype(BF16)
    return hi, (a - hi.astype(F32)).astype(BF16)


def kernel(
    anchor,
    diff,
    cour,
    parent,
    nest,
    pout,
    nout,
    work,
    res,
    pv,
    prow_in,
    pcol,
    pcol_in,
    item,
    item_in,
    wecol,
    strip,
    strip_in,
    edge,
    edge_in,
    ghost,
    fine,
    coef,
    triple,
    gcol,
    gcol_in,
    grow,
    grow_in,
    tall,
    col_fix,
    fix_w,
    fix_e,
    avg,
    slabs0,
    slabs1,
    slabs2,
    slab_out,
    canvas0,
    canvas1,
    canvas2,
    window,
    adv,
    tab,
    row_sem,
    local_sem,
    halo_sem,
    item_sem,
    strip_sem,
    edge_sem,
    slab_sem,
    canvas_sem,
    pair_sem,
):
    slabs = (slabs0, slabs1, slabs2)
    canvas = (canvas0, canvas1, canvas2)
    g = lax.axis_index("grp")
    d = lax.axis_index("dev")
    core = lax.rem(g, 2)
    row0 = g * TR
    col0 = d * TC
    lane = iota((1, 128), 1)

    own_parent = pltpu.make_async_copy(parent, pv, local_sem.at[0])
    own_parent.start()
    own_nest = [pltpu.make_async_copy(nest.at[:, r, :], work.at[3 + r], row_sem.at[r]) for r in range(NR)]
    for cp in own_nest:
        cp.start()
    barrier = pltpu.get_barrier_semaphore()
    for k in range(1, G):
        pl.semaphore_signal(barrier, inc=1, device_id={"grp": lax.rem(g + k, G)}, device_id_type=MESH)
    for k in range(1, D):
        pl.semaphore_signal(barrier, inc=1, device_id={"dev": lax.rem(d + k, D)}, device_id_type=MESH)

    for cp in own_nest:
        cp.wait()
    pl.semaphore_wait(barrier, G + D - 2)

    sends = []
    up_g, dn_g = lax.rem(g + 1, G), lax.rem(g + G - 1, G)
    up_d, dn_d = lax.rem(d + 1, D), lax.rem(d + D - 1, D)

    def halo(src, dst, i, axis, target):
        return remote(src, dst, halo_sem.at[0, i], halo_sem.at[1, i], axis, target)

    nest_halo = [
        halo(work.at[pl.ds(NR, 3)], work.at[pl.ds(0, 3)], 4, "dev", up_d),
        halo(work.at[pl.ds(3, 3)], work.at[pl.ds(NR + 3, 3)], 5, "dev", dn_d),
    ]
    parent_halo = [
        halo(parent.at[:, pl.ds(TR - 1, 1), :], prow_in.at[0, :, pl.ds(0, 1), :], 0, "grp", up_g),
        halo(parent.at[:, pl.ds(0, 1), :], prow_in.at[1, :, pl.ds(0, 1), :], 1, "grp", dn_g),
        halo(pcol.at[1], pcol_in.at[0], 2, "dev", up_d),
        halo(pcol.at[0], pcol_in.at[1], 3, "dev", dn_d),
    ]
    line_halo = [
        halo(gcol.at[pl.ds(TR - 8, 8)], gcol_in.at[0], 6, "grp", up_g),
        halo(gcol.at[pl.ds(0, 8)], gcol_in.at[1], 7, "grp", dn_g),
        halo(grow, grow_in.at[0], 8, "dev", up_d),
        halo(grow, grow_in.at[1], 9, "dev", dn_d),
    ]
    for cp in nest_halo + parent_halo[:2]:
        cp.start()

    key = [(anchor[0, n] >> 8) * 8 + (anchor[1, n] >> 8) for n in range(NESTS)]
    band_row = lax.div(g, 4)
    for b in range(8):
        found = jnp.int32(0)
        for n in range(NESTS):
            found = jnp.where(key[n] == band_row * 8 + b, n, found)
        tab[b] = found
    other = jnp.int32(0)
    for n in range(NESTS):
        other = jnp.where(key[n] == (1 - band_row) * 8 + lax.div(d, 2), n, other)
    mine = tab[lax.div(d, 2)]
    odd = lax.rem(d, 2)
    beside = tab[jnp.clip(lax.div(d, 2) - 1 + 2 * odd, 0, 7)]

    r_m, q_m = anchor[0, mine], anchor[1, mine]
    west_m = q_m - 1 - col0
    east_m = q_m + FP - col0
    is_west = (west_m >= 0) & (west_m < TC)
    is_east = (east_m >= 0) & (east_m < TC)
    pick = jnp.where(is_west, west_m, jnp.where(is_east, east_m, 0))
    q_b = anchor[1, beside]
    beside_on = jnp.where(odd == 1, q_b == col0 + TC, q_b + FP == col0)

    south_m = r_m - 1 - row0
    north_m = r_m + FP - row0
    is_south = (south_m >= 0) & (south_m < TR)
    is_north = (north_m >= 0) & (north_m < TR)
    row_pick = jnp.where(is_south, south_m, jnp.where(is_north, north_m, 0))
    r_o, q_o = anchor[0, other], anchor[1, other]
    low = band_row == 0
    other_on = jnp.where(low, r_o == row0 + TR, r_o + FP == row0)

    own_parent.wait()

    def gather(c, carry):
        first, last, picked, row_m, row_o = carry
        x = pv[c]
        here = lane == c
        first = jnp.where(here, pltpu.roll(x, c, 1), first)
        last = jnp.where(here, pltpu.roll(x, c + 1, 1), last)
        picked = jnp.where(here, pltpu.roll(x, (c - pick) & 127, 1), picked)
        sub = iota((C, 128), 0) == c
        row_m = jnp.where(sub, pv[c, pl.ds(row_pick, 1), :], row_m)
        edge_row = jnp.where(low, x[TR - 1 : TR], x[0:1])
        row_o = jnp.where(sub, edge_row, row_o)
        return first, last, picked, row_m, row_o

    zero_col = jnp.zeros((TR, 128), F32)
    zero_row = jnp.zeros((C, 128), F32)
    first, last, picked, row_m, row_o = lax.fori_loop(
        0, C, gather, (zero_col, zero_col, zero_col, zero_row, zero_row)
    )
    pcol[0] = first
    pcol[1] = last
    for cp in parent_halo[2:]:
        cp.start()
    side = jnp.where(odd == 1, last, first)
    place_m = (mine & 1) * 48 + jnp.where(is_west, 0, C)
    place_b = (beside & 1) * 48 + jnp.where(odd == 1, 0, C)
    cols_m = pltpu.roll(picked, place_m, 1)
    cols_b = pltpu.roll(side, place_b, 1)
    span_m = lane + (q_m - col0)
    span_o = lane + (q_o - col0)
    rows_m = jnp.where((span_m >= 0) & (span_m < TC), pltpu.roll(row_m, (col0 - q_m) & 127, 1), 0.0)
    rows_o = jnp.where((span_o >= 0) & (span_o < TC), pltpu.roll(row_o, (col0 - q_o) & 127, 1), 0.0)
    for t in range(G):
        a_m = jnp.where((mine >> 1 == t) & (is_west | is_east), 1, 0)
        a_b = jnp.where((beside >> 1 == t) & beside_on, 1, 0)
        item[t, pl.ds(0, TR), :] = jnp.where(a_m == 1, cols_m, 0.0) + jnp.where(a_b == 1, cols_b, 0.0)
        for a in range(2):
            s_m = jnp.where((mine == 2 * t + a) & (is_south | is_north), 1, 0)
            s_o = jnp.where((other == 2 * t + a) & other_on, 1, 0)
            item[t, pl.ds(TR + C * a, C), :] = jnp.where(s_m == 1, rows_m, 0.0) + jnp.where(
                s_o == 1, rows_o, 0.0
            )

    for k in range(1, G):
        t = lax.rem(g + k, G)
        cp = remote(item.at[t], item_in.at[g], item_sem.at[0, k], item_sem.at[1, k], "grp", t)
        cp.start()
        sends.append(cp)
    item_in[g] = item[g]

    lanes = [jnp.zeros((1, 128), F32)] * 5
    for c in range(C):
        kx, ky = 3.0 * diff[0, c], 3.0 * diff[1, c]
        ax, ay = cour[0, c], cour[1, c]
        here = (lane == c) | (lane == 32 + c)
        for i, v in enumerate((1.0 - 2.0 * kx - 2.0 * ky - ax - ay, kx, kx + ax, ky, ky + ay)):
            coef[i, pl.ds(c, 1), :] = jnp.full((1, 128), v, F32)
            lanes[i] = jnp.where(here, v, lanes[i])

    for cp in nest_halo:
        cp.wait()

    off = iota((NC, TC), 0) - 3 * iota((NC, TC), 1)
    collect = one_hot((off >= 0) & (off < 3))
    first_dev, last_dev = d == 0, d == D - 1
    tiles = range(3)

    def substeps(j, a):
        plane = pl.ds(pl.multiple_of(C * a + 8 * j, 8), 8)
        k_c, k_x, k_w, k_y, k_s = (coef[i, pl.ds(8 * j, 8), :] for i in range(5))
        def keep(w, row):
            if w == 2:
                return [jnp.where(first_dev, 0.0, row[i]) for i in tiles]
            if w == NR + 3:
                return [jnp.where(last_dev, 0.0, row[i]) for i in tiles]
            return row

        def advance(below, row, above):
            right = [0.0] + [pltpu.roll(v, 1, 1) for v in row]
            left = [pltpu.roll(v, 127, 1) for v in row] + [0.0]
            return [
                k_c * row[i]
                + k_x * jnp.where(lane == 127, left[i + 1], left[i])
                + k_w * jnp.where(lane == 0, right[i], right[i + 1])
                + k_y * above[i]
                + k_s * below[i]
                for i in tiles
            ]

        levels = [{}, {}, {}]
        acc = None
        for w in range(NR + 6):
            levels[0][w] = keep(w, [work[w, plane, pl.ds(128 * i, 128)] for i in tiles])
            for n in range(3):
                v = w - n - 1
                if v <= n or v >= NR + 5 - n:
                    continue
                src = levels[n]
                made = advance(src[v - 1], src[v], src[v + 1])
                del src[v - 1]
                if n < 2:
                    levels[n + 1][v] = keep(v, made)
                    continue
                for i in tiles:
                    res[v - 3, plane, pl.ds(128 * i, 128)] = made[i]
                acc = made if (v - 3) % 3 == 0 else [x + y for x, y in zip(acc, made)]
                if (v - 3) % 3 == 2:
                    at = pl.ds(pl.multiple_of(64 * a + 8 * ((v - 3) // 3), 8), 8)
                    for i in tiles:
                        triple[at, pl.ds(128 * i, 128)] = acc[i]

    pair = g + 1 - 2 * core

    def slab_copy(j, k, t, mine_g):
        return remote(
            avg.at[j, :, pl.ds(4 * (lax.rem(t, 2)), 4)],
            slabs[j].at[pl.ds(2 * mine_g, 2)],
            slab_sem.at[0, j, k],
            slab_sem.at[1, j, k],
            "grp",
            t,
        )

    def canvas_copy(j, k, t, mine_d):
        return remote(
            slab_out.at[j, k],
            canvas[j].at[8 + mine_d, core],
            canvas_sem.at[0, j, k],
            canvas_sem.at[1, j, k],
            "dev",
            t,
        )

    def pair_copy(j, half):
        block = canvas[j].at[pl.ds(8, D), half]
        return remote(block, block, pair_sem.at[0, j], pair_sem.at[1, j], "grp", pair)

    def to_groups(j):
        for k in range(1, G):
            cp = slab_copy(j, k, lax.rem(g + k, G), g)
            cp.start()
            sends.append(cp)
        slabs[j][pl.ds(2 * g, 2)] = avg[j, :, pl.ds(4 * core, 4)]

    def to_columns(j):
        for k in range(1, G):
            slab_copy(j, k, g, lax.rem(g + G - k, G)).wait_recv()
        for k in range(1, D):
            t = lax.rem(d + k, D)
            slab_out[j, k] = slabs[j][tab[lax.div(t, 2)]]
            cp = canvas_copy(j, k, t, d)
            cp.start()
            sends.append(cp)
        canvas[j][8 + d, core] = slabs[j][mine]

    def to_pair(j):
        for k in range(1, D):
            canvas_copy(j, k, d, lax.rem(d + D - k, D)).wait_recv()
        cp = pair_copy(j, core)
        cp.start()
        sends.append(cp)

    own_row = jnp.clip(row0 - r_m, -TR, FP) + TR
    shift = (q_m - col0) & 127
    tile_row = iota((TR, 128), 0) + (row0 - r_m)
    tile_col = iota((TR, 128), 1) + (col0 - q_m)
    covered = (tile_row >= 0) & (tile_row < FP) & (tile_col >= 0) & (tile_col < FP)
    rows_of = [c.reshape(256, 8, TC) for c in canvas]
    outs = []

    def place(j):
        pair_copy(j, 1 - core).wait_recv()
        window[...] = rows_of[j][pl.ds(own_row, TR)].reshape(8 * TR, TC)
        for i in range(8):
            c = 8 * j + i
            under = pltpu.roll(window[pl.ds(i, TR, stride=8), :], shift, 1)
            fix = col_fix[...]
            under += jnp.where(lane == at_w, pltpu.roll(fix, (at_w - c) & 127, 1), 0.0)
            under += jnp.where(lane == at_e, pltpu.roll(fix, (at_e - 32 - c) & 127, 1), 0.0)
            under += jnp.where(tile == row_at, row_fix[c : c + 1], 0.0)
            adv[c] = jnp.where(covered, under, adv[c])
        cp = pltpu.make_async_copy(adv.at[pl.ds(8 * j, 8)], pout.at[pl.ds(8 * j, 8)], local_sem.at[1 + j])
        cp.start()
        outs.append(cp)

    def compute(j):
        def one(a, _):
            substeps(j, a)
            return 0

        lax.fori_loop(0, 2, one, 0)
        mean = select_dot(split2(triple[...]), collect) * (1.0 / 9.0)
        avg[j] = mean.reshape(2, 8, 8, TC)
        to_groups(j)

    compute(0)
    compute(1)
    compute(2)
    to_columns(0)

    for k in range(1, G):
        s = lax.rem(g + G - k, G)
        remote(item.at[s], item_in.at[s], item_sem.at[0, k], item_sem.at[1, k], "grp", s).wait_recv()
    wecol[pl.ds(0, LEAD), :] = jnp.zeros((LEAD, 128), F32)
    wecol[pl.ds(LEAD + G * TR, 32), :] = jnp.zeros((32, 128), F32)
    south = [jnp.zeros((C, 128), F32)] * 2
    north = [jnp.zeros((C, 128), F32)] * 2
    r_own = [anchor[0, 2 * g + a] for a in range(2)]
    for s in range(G):
        wecol[pl.ds(LEAD + s * TR, TR), :] = item_in[s, pl.ds(0, TR), :]
        for a in range(2):
            got = item_in[s, pl.ds(TR + C * a, C), :]
            below = r_own[a] - 1 - s * TR
            above = r_own[a] + FP - s * TR
            south[a] = south[a] + jnp.where((below >= 0) & (below < TR), got, 0.0)
            north[a] = north[a] + jnp.where((above >= 0) & (above < TR), got, 0.0)
    for a in range(2):
        edge[0, pl.ds(C * a, C), :] = south[a]
        edge[1, pl.ds(C * a, C), :] = north[a]

    def strip_of(t):
        parts = [wecol[pl.ds(LEAD - 1 + r_own[a] + 8 * t, 16), :] for a in range(2)]
        return jnp.where(lane < 48, parts[0], parts[1])

    for k in range(1, D):
        t = lax.rem(d + k, D)
        strip[k] = strip_of(t)
        cp = remote(strip.at[k], strip_in.at[k], strip_sem.at[0, k], strip_sem.at[1, k], "dev", t)
        cp.start()
        sends.append(cp)
    strip_in[0] = strip_of(d)

    for e, end in ((0, 0), (1, D - 1)):

        @pl.when(d != end)
        def _(e=e, end=end):
            remote(edge.at[e], edge_in.at[d], edge_sem.at[0, e], edge_sem.at[1, d], "dev", end).start()

    to_columns(1)

    for cp in parent_halo:
        cp.wait()
    at_w, at_e = q_m - col0, q_m + FP - 1 - col0
    at_s, at_n = r_m - row0, r_m + FP - 1 - row0
    from_w = jnp.where(d == 0, 0.0, pcol_in[0])
    from_e = jnp.where(d == D - 1, 0.0, pcol_in[1])
    line_w = jnp.where(at_w == 0, from_w, picked)
    line_e = jnp.where(at_e == TC - 1, from_e, picked)
    gcol[...] = jnp.where(lane < 32, line_w, pltpu.roll(line_e, 32, 1))
    has_s = (at_s >= 0) & (at_s < TR)
    from_s = jnp.where(g == 0, 0.0, prow_in[0, :, 0, :])
    from_n = jnp.where(g == G - 1, 0.0, prow_in[1, :, 0, :])
    grow[...] = jnp.where(at_s == 0, from_s, jnp.where(at_n == TR - 1, from_n, row_m))
    for cp in line_halo:
        cp.start()
    to_columns(2)

    tile = iota((TR, 128), 0)

    def parent_step(c, _):
        mid = pv[c]
        kx, ky = diff[0, c], diff[1, c]
        ax, ay = cour[0, c], cour[1, c]
        gw = jnp.where(d == 0, 0.0, pltpu.roll(pcol_in[0], (128 - c) & 127, 1))
        ge = jnp.where(d == D - 1, 0.0, pltpu.roll(pcol_in[1], 127 - c, 1))
        gs = jnp.where(g == 0, 0.0, prow_in[0, c, 0:1, :])
        gn = jnp.where(g == G - 1, 0.0, prow_in[1, c, 0:1, :])
        west = jnp.where(lane == 0, gw, pltpu.roll(mid, 1, 1))
        east = jnp.where(lane == 127, ge, pltpu.roll(mid, 127, 1))
        below = jnp.where(tile == 0, gs, pltpu.roll(mid, 1, 0))
        above = jnp.where(tile == TR - 1, gn, pltpu.roll(mid, TR - 1, 0))
        adv[c] = (
            mid * (1.0 - 2.0 * kx - 2.0 * ky - ax - ay)
            + kx * east
            + (kx + ax) * west
            + ky * above
            + (ky + ay) * below
        )
        return 0

    lax.fori_loop(0, C, parent_step, 0)


    for cp in line_halo:
        cp.wait()
    column = jnp.concatenate([gcol_in[0], gcol[...], gcol_in[1]], axis=0)
    for k in range(3):
        tall[pl.ds(k, TR + 16, stride=3), :] = column
    tall_row = iota((3 * (TR + 16), 128), 0) + 3 * (row0 - r_m - 8)
    inside = (tall_row >= 0) & (tall_row < NC)
    l_c, l_x, l_w, l_y, l_s = lanes
    size = 3 * (TR + 16)

    def down(u, add):
        if u is not None:
            add += l_c * u + l_y * pltpu.roll(u, size - 1, 0) + l_s * pltpu.roll(u, 1, 0)
        return jnp.where(inside, add, 0.0)

    w_lane = lane < 32
    tall[...] = sum(response(tall[...], jnp.where(w_lane, l_w, l_x), jnp.where(w_lane, l_x, l_w), down))
    col_fix[...] = sum(tall[pl.ds(24 + k, TR, stride=3), :] for k in range(3)) * (1.0 / 9.0)

    wide = 512
    wide_off = iota((TC, wide), 1) - 64 - 3 * iota((TC, wide), 0)
    to_wide = [one_hot((wide_off + o >= 0) & (wide_off + o < 3)) for o in (NC, 0, -NC)]
    row = sum(
        select_dot(split3(v), m) for v, m in zip((grow_in[0], grow[...], grow_in[1]), to_wide)
    )
    wide_col = iota((C, wide), 1) - 64 + 3 * (col0 - q_m)
    within = (wide_col >= 0) & (wide_col < NC)
    c_c, c_x, c_w, c_y, c_s = (jnp.concatenate([coef[i]] * 4, axis=1) for i in range(5))

    def across(u, add):
        if u is not None:
            add += c_c * u + c_x * pltpu.roll(u, wide - 1, 1) + c_w * pltpu.roll(u, 1, 1)
        return jnp.where(within, add, 0.0)

    strip_sum = sum(response(row, jnp.where(has_s, c_s, c_y), jnp.where(has_s, c_y, c_s), across))
    back = iota((wide, TC), 0) - 64 - 3 * iota((wide, TC), 1)
    row_fix = select_dot(split2(strip_sum), one_hot((back >= 0) & (back < 3))) * (1.0 / 9.0)
    row_at = jnp.where(has_s, at_s, at_n)

    to_pair(0)

    for k in range(1, D):
        remote(strip.at[k], strip_in.at[k], strip_sem.at[0, k], strip_sem.at[1, k], "dev", d).wait_recv()
    total = strip_in[0]
    for k in range(1, D):
        total = total + strip_in[k]
    ghost[...] = jnp.transpose(jnp.concatenate([total, jnp.zeros((112, 128), F32)], axis=0))

    spread_off = iota((128, 128), 1) - 3 * iota((128, 128), 0)
    fine_ghost = select_dot(split3(ghost[...]), one_hot((spread_off >= 0) & (spread_off < 3)))
    open_rows = ((lane >= 3) | (d != 0)) & ((lane < NR + 3) | (d != D - 1)) & (lane < NR + 6)
    n_c, n_x, n_w, n_y, n_s = (jnp.concatenate([coef[i]] * 2, axis=0) for i in range(5))

    def along(u, add):
        if u is not None:
            add += n_c * u + n_y * pltpu.roll(u, 127, 1) + n_s * pltpu.roll(u, 1, 1)
        return jnp.where(open_rows, add, 0.0)

    pack_off = iota((128, 128), 1) - 3 * (iota((128, 128), 0) - 3)
    packed = []
    for side, near, far in ((0, n_w, n_x), (1, n_x, n_w)):
        g_side = jnp.concatenate([fine_ghost[48 * a + C * side : 48 * a + C * side + C] for a in range(2)], axis=0)
        lines = response(g_side, near, far, along)
        packed.append(
            sum(
                select_dot(split2(v), one_hot(pack_off == (k if side == 0 else 2 - k)))
                for k, v in enumerate(lines)
            )
        )
    fix_w[...] = packed[0]
    fix_e[...] = packed[1]

    def fix_cols(t, _):
        plane = pl.ds(pl.multiple_of(8 * t, 8), 8)
        w_fix, e_fix = fix_w[plane, :], fix_e[plane, :]
        for f in range(NR):
            res[f, plane, pl.ds(0, 128)] += jnp.where(lane < 3, pltpu.roll(w_fix, (128 - 3 * f) % 128, 1), 0.0)
            res[f, plane, pl.ds(256, 128)] += jnp.where(lane >= 125, pltpu.roll(e_fix, (125 - 3 * f) % 128, 1), 0.0)
        return 0

    lax.fori_loop(0, 6, fix_cols, 0)

    def store_rows(some):
        for r in some:
            cp = pltpu.make_async_copy(res.at[r], nout.at[:, r, :], row_sem.at[r])
            cp.start()
            outs.append(cp)

    store_rows(range(3, NR - 3))
    to_pair(1)
    to_pair(2)
    place(0)

    for e, end in ((0, 0), (1, D - 1)):

        @pl.when(d == end)
        def _(e=e, end=end):
            whole = edge[e]
            for k in range(1, D):
                s = (end + k) % D
                remote(edge.at[e], edge_in.at[s], edge_sem.at[0, e], edge_sem.at[1, s], "dev", end).wait_recv()
            for k in range(1, D):
                whole = whole + edge_in[(end + k) % D]
            off = iota((TC, NC), 1) - 3 * iota((TC, NC), 0)
            spread = jnp.where((off >= 0) & (off < 3), 1.0, 0.0).astype(BF16)
            fine[...] = sum(
                jnp.dot(part, spread, preferred_element_type=F32) for part in split3(whole)
            )

        @pl.when(d != end)
        def _(e=e, end=end):
            remote(edge.at[e], edge_in.at[d], edge_sem.at[0, e], edge_sem.at[1, d], "dev", end).wait_send()


    for e, end in ((0, 0), (1, D - 1)):

        @pl.when(d == end)
        def _(e=e):
            n3 = [jnp.concatenate([v] * 3, axis=1) for v in (n_c, n_x, n_w, n_y, n_s)]
            at = iota((PLANES, NC), 1)

            def over(u, add):
                if u is None:
                    return add
                right = jnp.where(at == NC - 1, 0.0, pltpu.roll(u, NC - 1, 1))
                left = jnp.where(at == 0, 0.0, pltpu.roll(u, 1, 1))
                return n3[0] * u + n3[1] * right + n3[2] * left + add

            near, far = (n3[4], n3[3]) if e == 0 else (n3[3], n3[4])
            for k, v in enumerate(response(fine[...], near, far, over)):
                res[k if e == 0 else NR - 1 - k] += v

    store_rows([0, 1, 2, NR - 3, NR - 2, NR - 1])
    place(1)
    place(2)
    for cp in sends:
        cp.wait_send()
    for cp in outs:
        cp.wait()


def shards(parent, nest, anchor, diffusion, courant):
    any_space = pl.BlockSpec(memory_space=pl.ANY)
    scalars = pl.BlockSpec(memory_space=pltpu.SMEM)
    dma = pltpu.SemaphoreType.DMA
    vmem = pltpu.VMEM
    pout, nout = pl.pallas_call(
        kernel,
        out_shape=(
            jax.ShapeDtypeStruct((C, TR, TC), F32),
            jax.ShapeDtypeStruct((PLANES, NR, NC), F32),
        ),
        in_specs=[scalars] * 3 + [any_space] * 2,
        out_specs=(any_space, any_space),
        scratch_shapes=[
            vmem((NR + 6, PLANES, NC), F32),
            vmem((NR, PLANES, NC), F32),
            vmem((C, TR, TC), F32),
            vmem((2, C, 8, TC), F32),
            vmem((2, TR, 128), F32),
            vmem((2, TR, 128), F32),
            vmem((G, TR + PLANES, 128), F32),
            vmem((G, TR + PLANES, 128), F32),
            vmem((LEAD + G * TR + 32, 128), F32),
            vmem((D, 16, 128), F32),
            vmem((D, 16, 128), F32),
            vmem((2, PLANES, 128), F32),
            vmem((D, PLANES, 128), F32),
            vmem((128, 128), F32),
            vmem((PLANES, NC), F32),
            vmem((5, C, 128), F32),
            vmem((128, NC), F32),
            vmem((TR, 128), F32),
            vmem((2, 8, 128), F32),
            vmem((C, 128), F32),
            vmem((2, C, 128), F32),
            vmem((3 * (TR + 16), 128), F32),
            vmem((TR, 128), F32),
            vmem((PLANES, 128), F32),
            vmem((PLANES, 128), F32),
            vmem((3, 2, 8, 8, TC), F32),
            *[vmem((NESTS, 4, 8, TC), F32)] * 3,
            vmem((3, D, 4, 8, TC), F32),
            *[vmem((32, 2, 4, 8, TC), F32)] * 3,
            vmem((8 * TR, TC), F32),
            vmem((C, TR, TC), F32),
            pltpu.SMEM((8,), I32),
            dma((NR,)),
            dma((4,)),
            dma((2, 10)),
            dma((2, G)),
            dma((2, D)),
            dma((2, D)),
            dma((2, 3, G)),
            dma((2, 3, D)),
            dma((2, 3)),
        ],
        compiler_params=pltpu.CompilerParams(
            collective_id=0, has_side_effects=True, vmem_limit_bytes=60 * 1024 * 1024
        ),
    )(anchor.T, diffusion, courant, parent, nest.reshape(PLANES, NR, NC))
    return pout, nout.reshape(2, C, NR, NC)


def solution(mesh):
    placed = (P(None, "grp", "dev"), P("grp", None, "dev", None), P(), P(), P())
    return jax.shard_map(
        shards,
        mesh=mesh,
        in_specs=placed,
        out_specs=(P(None, "grp", "dev"), P("grp", None, "dev", None)),
        check_vma=False,
    )
```

time: 58 us -> 53.7 us (0.926)
  Pallas kernels: 50.3 us -> 47.9 us
  local copies, waits for them, and re-layouts: 6.81 us -> 4.89 us
    pallas_call x1, Pallas kernels: 50.3 us -> 47.9 us  [shards(): pl.pallas_call(kernel, out_shape=(jax.ShapeDtypeStruct((C, TR, TC), F32),...]
    unnamed x11 -> x2, local copies, waits for them, and re-layouts: 6.81 us -> 4.89 us
where the time goes in v3:
time: 53.7 us; the launch traced here: 53.4 us
  Pallas kernels  47.9 us (89%)
  local copies, waits for them, and re-layouts  4.89 us (9%)
  between operations  0.64 us (1%)
    pallas_call x1, Pallas kernels, shards(): pl.pallas_call(kernel, out_shape=(jax.ShapeDtypeStruct((C, TR, TC), F32),...  47.9 us
    unnamed x2, local copies, waits for them, and re-layouts  4.89 us

profile of v3, /device:TPU:1, one launch (start us, length us, event | category | flops | bytes accessed | tf_op | source)
XLA Modules:
  0.0 53.4 jit_solution(2992697053092052636)
XLA Ops:
  0.6 47.9 %shard_map.68 = (f32[24,64,128]{2,1,0:T(8,128)}, f32[48,24,384]{2,1,0:T(8,128)}) custom-call(s32[2,16]{1,0:T(2,128)} %bitcast.5, f32[2,24]{1,0:T(2,128)} %diff.1, f32[2,24]{1,0:T(2,128)} %cour.1, f32[24,64,128]{2,1,0:T(8,128)} %parent.1, f32[48,24,384]{2,1,0:T(8,128)} %bitcast.4), custom_call_target="tpu_custom_call" | custom-call | tf_op jit(solution)/shard_map/pallas_call | solution.py:641
  48.5 2.1 %copy.9 = f32[24,64,128]{2,1,0:T(8,128)} copy(f32[24,64,128]{2,1,0:T(8,128)} %get-tuple-element.8) | data formatting | bytes 1572864
  50.6 2.8 %copy.10 = f32[2,24,24,384]{3,2,1,0:T(8,128)} copy(f32[2,24,24,384]{3,2,1,0:T(8,128)} %bitcast.3) | data formatting | bytes 3538944

commit v4 on v3

--- a/solution.py
+++ b/solution.py
@@ -405,9 +405,8 @@
         to_groups(j)
 
     compute(0)
+
     compute(1)
-    compute(2)
-    to_columns(0)
 
     for k in range(1, G):
         s = lax.rem(g + G - k, G)
@@ -447,7 +446,8 @@
         def _(e=e, end=end):
             remote(edge.at[e], edge_in.at[d], edge_sem.at[0, e], edge_sem.at[1, d], "dev", end).start()
 
-    to_columns(1)
+
+    compute(2)
 
     for cp in parent_halo:
         cp.wait()
@@ -464,6 +464,11 @@
     grow[...] = jnp.where(at_s == 0, from_s, jnp.where(at_n == TR - 1, from_n, row_m))
     for cp in line_halo:
         cp.start()
+
+    to_columns(0)
+
+    to_columns(1)
+
     to_columns(2)
 
     tile = iota((TR, 128), 0)
@@ -641,10 +646,10 @@
     pout, nout = pl.pallas_call(
         kernel,
         out_shape=(
-            jax.ShapeDtypeStruct((C, TR, TC), F32),
-            jax.ShapeDtypeStruct((PLANES, NR, NC), F32),
+            pltpu.VMEM((C, TR, TC), F32),
+            pltpu.VMEM((PLANES, NR, NC), F32),
         ),
-        in_specs=[scalars] * 3 + [any_space] * 2,
+        in_specs=[scalars] * 3 + [pl.BlockSpec(memory_space=pltpu.HBM)] * 2,
         out_specs=(any_space, any_space),
         scratch_shapes=[
             vmem((NR + 6, PLANES, NC), F32),
@@ -690,9 +695,9 @@
             dma((2, 3)),
         ],
         compiler_params=pltpu.CompilerParams(
-            collective_id=0, has_side_effects=True, vmem_limit_bytes=60 * 1024 * 1024
+            collective_id=0, has_side_effects=True, vmem_limit_bytes=52 * 1024 * 1024
         ),
-    )(anchor.T, diffusion, courant, parent, nest.reshape(PLANES, NR, NC))
+    )(anchor.T, diffusion, courant, pltpu.with_memory_space_constraint(parent, pltpu.HBM), pltpu.with_memory_space_constraint(nest.reshape(PLANES, NR, NC), pltpu.HBM))
     return pout, nout.reshape(2, C, NR, NC)
 
 

time: 53.7 us -> 45.7 us (0.85)
  the two profiles are of different devices: /device:TPU:1 before, /device:TPU:3 now
where the time goes in v4:
time: 45.7 us; the launch traced here: 45.5 us
  Pallas kernels  42.8 us (94%)
  local copies, waits for them, and re-layouts  2.09 us (5%)
  between operations  0.64 us (1%)
    pallas_call x1, Pallas kernels, shards(): pl.pallas_call(kernel, out_shape=(pltpu.VMEM((C, TR, TC), F32), pltpu.VME...  42.8 us
    unnamed x2, local copies, waits for them, and re-layouts  2.09 us

profile of v4, /device:TPU:3, one launch (start us, length us, event | category | flops | bytes accessed | tf_op | source)
XLA Modules:
  0.0 45.5 jit_solution(14746420304396615452)
XLA Ops:
  0.6 42.8 %shard_map.68 = (f32[24,64,128]{2,1,0:T(8,128)S(1)}, f32[48,24,384]{2,1,0:T(8,128)S(1)}) custom-call(s32[2,16]{1,0:T(2,128)} %bitcast.5, f32[2,24]{1,0:T(2,128)} %diff.1, f32[2,24]{1,0:T(2,128)} %cour.1, f32[24,64,128]{2,1,0:T(8,128)} %parent.1, f32[48,24,384]{2,1,0:T(8,128)} %bitcast.4), custom_call_target="tpu_custom_call" | custom-call | tf_op jit(solution)/shard_map/pallas_call | solution.py:646
  43.4 0.9 %copy.9 = f32[24,64,128]{2,1,0:T(8,128)} copy(f32[24,64,128]{2,1,0:T(8,128)S(1)} %get-tuple-element.6) | data formatting | bytes 1572864
  44.3 1.2 %copy.10 = f32[2,24,24,384]{3,2,1,0:T(8,128)} copy(f32[2,24,24,384]{3,2,1,0:T(8,128)S(1)} %bitcast.3) | data formatting | bytes 3538944

commit v5 on v4

--- a/solution.py
+++ b/solution.py
@@ -406,8 +406,6 @@
 
     compute(0)
 
-    compute(1)
-
     for k in range(1, G):
         s = lax.rem(g + G - k, G)
         remote(item.at[s], item_in.at[s], item_sem.at[0, k], item_sem.at[1, k], "grp", s).wait_recv()
@@ -447,7 +445,7 @@
             remote(edge.at[e], edge_in.at[d], edge_sem.at[0, e], edge_sem.at[1, d], "dev", end).start()
 
 
-    compute(2)
+    compute(1)
 
     for cp in parent_halo:
         cp.wait()
@@ -464,6 +462,8 @@
     grow[...] = jnp.where(at_s == 0, from_s, jnp.where(at_n == TR - 1, from_n, row_m))
     for cp in line_halo:
         cp.start()
+
+    compute(2)
 
     to_columns(0)
 

time: 45.7 us -> 43.8 us (0.958)
  the two profiles are of different devices: /device:TPU:3 before, /device:TPU:1 now
where the time goes in v5:
time: 43.8 us; the launch traced here: 43.6 us
  Pallas kernels  40.9 us (93%)
  local copies, waits for them, and re-layouts  2.09 us (5%)
  between operations  0.64 us (1%)
    pallas_call x1, Pallas kernels, shards(): pl.pallas_call(kernel, out_shape=(pltpu.VMEM((C, TR, TC), F32), pltpu.VME...  40.9 us
    unnamed x2, local copies, waits for them, and re-layouts  2.09 us

profile of v5, /device:TPU:1, one launch (start us, length us, event | category | flops | bytes accessed | tf_op | source)
XLA Modules:
  0.0 43.6 jit_solution(17062122461381320530)
XLA Ops:
  0.6 40.9 %shard_map.68 = (f32[24,64,128]{2,1,0:T(8,128)S(1)}, f32[48,24,384]{2,1,0:T(8,128)S(1)}) custom-call(s32[2,16]{1,0:T(2,128)} %bitcast.5, f32[2,24]{1,0:T(2,128)} %diff.1, f32[2,24]{1,0:T(2,128)} %cour.1, f32[24,64,128]{2,1,0:T(8,128)} %parent.1, f32[48,24,384]{2,1,0:T(8,128)} %bitcast.4), custom_call_target="tpu_custom_call" | custom-call | tf_op jit(solution)/shard_map/pallas_call | solution.py:646
  41.6 0.9 %copy.9 = f32[24,64,128]{2,1,0:T(8,128)} copy(f32[24,64,128]{2,1,0:T(8,128)S(1)} %get-tuple-element.6) | data formatting | bytes 1572864
  42.4 1.2 %copy.10 = f32[2,24,24,384]{3,2,1,0:T(8,128)} copy(f32[2,24,24,384]{3,2,1,0:T(8,128)S(1)} %bitcast.3) | data formatting | bytes 3538944

commit v6 on v5

--- a/solution.py
+++ b/solution.py
@@ -347,7 +347,7 @@
         return remote(block, block, pair_sem.at[0, j], pair_sem.at[1, j], "grp", pair)
 
     def to_groups(j):
-        for k in range(1, G):
+        for k in (4, 3, 5, 2, 6, 7, 1):
             cp = slab_copy(j, k, lax.rem(g + k, G), g)
             cp.start()
             sends.append(cp)
@@ -356,7 +356,7 @@
     def to_columns(j):
         for k in range(1, G):
             slab_copy(j, k, g, lax.rem(g + G - k, G)).wait_recv()
-        for k in range(1, D):
+        for k in (10, 9, 11, 6, 14, 8, 2, 5, 7, 13, 15, 3, 12, 4, 1):
             t = lax.rem(d + k, D)
             slab_out[j, k] = slabs[j][tab[lax.div(t, 2)]]
             cp = canvas_copy(j, k, t, d)

time: 43.8 us -> 44.6 us (1.018)
  Pallas kernels: 40.9 us -> 41.7 us
    pallas_call x1, Pallas kernels: 40.9 us -> 41.7 us  [shards(): pl.pallas_call(kernel, out_shape=(pltpu.VMEM((C, TR, TC), F32), pltpu.VME...]
where the time goes in v6:
time: 44.6 us; the launch traced here: 44.5 us
  Pallas kernels  41.7 us (93%)
  local copies, waits for them, and re-layouts  2.09 us (5%)
  between operations  0.64 us (1%)
    pallas_call x1, Pallas kernels, shards(): pl.pallas_call(kernel, out_shape=(pltpu.VMEM((C, TR, TC), F32), pltpu.VME...  41.7 us
    unnamed x2, local copies, waits for them, and re-layouts  2.09 us

profile of v6, /device:TPU:1, one launch (start us, length us, event | category | flops | bytes accessed | tf_op | source)
XLA Modules:
  0.0 44.5 jit_solution(8160286765783406435)
XLA Ops:
  0.6 41.7 %shard_map.68 = (f32[24,64,128]{2,1,0:T(8,128)S(1)}, f32[48,24,384]{2,1,0:T(8,128)S(1)}) custom-call(s32[2,16]{1,0:T(2,128)} %bitcast.5, f32[2,24]{1,0:T(2,128)} %diff.1, f32[2,24]{1,0:T(2,128)} %cour.1, f32[24,64,128]{2,1,0:T(8,128)} %parent.1, f32[48,24,384]{2,1,0:T(8,128)} %bitcast.4), custom_call_target="tpu_custom_call" | custom-call | tf_op jit(solution)/shard_map/pallas_call | solution.py:646
  42.4 0.9 %copy.9 = f32[24,64,128]{2,1,0:T(8,128)} copy(f32[24,64,128]{2,1,0:T(8,128)S(1)} %get-tuple-element.6) | data formatting | bytes 1572864
  43.2 1.2 %copy.10 = f32[2,24,24,384]{3,2,1,0:T(8,128)} copy(f32[2,24,24,384]{3,2,1,0:T(8,128)S(1)} %bitcast.3) | data formatting | bytes 3538944
